TPU v7x, 256 devices: a whole 4x4x8 slice. The times are simulated.
256 devices in a mesh: px: 16 (over y, x), py: 16 (over z, core).
Axes of the slice: x: 4, y: 4, z: 8, core: 2. Of those that a mesh axis runs over, the one named last changes fastest.
Arguments:
- source: float32 [8, 512, 2048], P(None, 'px', 'py'), may hold values from -12 to 12
- coefficient: float32 [8, 512, 2048], P(None, 'px', 'py'), may hold values from 0.25 to 4
- strip_rows: int32 [16], replicated, may hold values from 1 to 72, 128 in all
Outputs:
- solution: float32 [8, 512, 2048], P(None, 'px', 'py')
Inputs may be any that keep to these rules, and one draw needn't show every extreme that they name: `strip_rows`: the entries sum to 128 and the largest is exactly 72.
All inputs are finite; a program needn't handle non-finite values.
Results may differ from a plain program's by a relative error of at most 0.00027.
Values sent between devices are 32-bit elements; how exact they have to be, the bound alone decides.
A program may use at most 128 MiB of HBM per device.

v0:
```python
import jax
import jax.numpy as jnp
from jax import lax
from jax.sharding import PartitionSpec as P

CYCLES = 2
PRE = 2
POST = 2
COARSE_SWEEPS = 6


relaxation = 0.8
z_coupling = 0.25


def extended(array, sides, width):
    for axis, dim in sides:
        peers, length = (lax.axis_size(axis), array.shape[dim])
        up = [(i, (i + 1) % peers) for i in range(peers - 1)]
        down = [(j, i) for i, j in up]
        last = lax.slice_in_dim(array, length - width, length, axis=dim)
        initial = lax.slice_in_dim(array, 0, width, axis=dim)
        before = lax.ppermute(last, axis, up)
        after = lax.ppermute(initial, axis, down)
        array = jnp.concatenate([before, array, after], axis=dim)
    return array


def pad_plain(values):
    return jnp.pad(values, ((0, 0), (1, 1), (1, 1)))


def extend(values, margin_width):
    return extended(values[None], (("px", 2), ("py", 3)), margin_width)[0]


def face_arrays(conduct, z_factor):
    padded = pad_plain(conduct)
    face_west = 0.5 * (conduct + padded[:, :-2, 1:-1])
    face_east = 0.5 * (conduct + padded[:, 2:, 1:-1])
    face_south = 0.5 * (conduct + padded[:, 1:-1, :-2])
    face_north = 0.5 * (conduct + padded[:, 1:-1, 2:])
    vertical = z_factor * 0.5 * (conduct[:-1] + conduct[1:])
    zero_layer = jnp.zeros_like(conduct[:1])
    face_down = jnp.concatenate([zero_layer, vertical], axis=0)
    face_up = jnp.concatenate([vertical, zero_layer], axis=0)
    diagonal = face_west + face_east + face_south + face_north + face_down + face_up
    return [face_west, face_east, face_south, face_north, face_down, face_up, diagonal]


def invert(diagonal, inside):
    safe_diag = jnp.where(inside, diagonal, 1.0)
    return jnp.where(inside, 1.0 / safe_diag, 0.0)


def update(values, values_pad, faces, source_term):
    face_west, face_east, face_south, face_north, face_down, face_up, diagonal, inverse = faces
    zero_layer = jnp.zeros_like(values[:1])
    value_down = jnp.concatenate([zero_layer, values[:-1]], axis=0)
    value_up = jnp.concatenate([values[1:], zero_layer], axis=0)
    beside = (
        face_west * values_pad[:, :-2, 1:-1]
        + face_east * values_pad[:, 2:, 1:-1]
        + face_south * values_pad[:, 1:-1, :-2]
        + face_north * values_pad[:, 1:-1, 2:]
        + face_down * value_down
        + face_up * value_up
    )
    return source_term - diagonal * values + beside


def relax_sweep(values, values_pad, faces, source_term):
    return values + relaxation * faces[7] * update(values, values_pad, faces, source_term)


def residual(values, source_term, faces_int):
    return update(values, extend(values, 1), faces_int, source_term)


def coarsen(values):
    layers, row_count, col_count = values.shape
    return 0.25 * values.reshape(layers, row_count // 2, 2, col_count // 2, 2).sum(axis=(2, 4))


def restrict(values):
    layers, row_count, col_count = values.shape
    return values.reshape(layers, row_count // 2, 2, col_count // 2, 2).sum(axis=(2, 4))


def prolong(values):
    return jnp.repeat(jnp.repeat(values, 2, axis=1), 2, axis=2)


def prepare(conduct, z_factor, margin_width):
    wide = extend(conduct, margin_width)
    faces_ext = face_arrays(wide, z_factor)
    faces_ext.append(invert(faces_ext[6], wide > 0.0))
    faces_int = [
        member[:, margin_width:-margin_width, margin_width:-margin_width] for member in faces_ext
    ]
    return (faces_int, faces_ext)


def smooth_level(values, source_term, faces_int, count):
    for sweep_index in range(count):
        values = relax_sweep(values, extend(values, 1), faces_int, source_term)
    return values


def to_strips(level_values, starts, most_rows):
    gathered = lax.all_gather(level_values, "px", axis=1, tiled=True)
    padded = jnp.pad(gathered, ((0, 0), (1, most_rows + 1), (0, 0)))

    def cut_strip(first_row):
        return lax.dynamic_slice_in_dim(padded, first_row, most_rows + 2, 1)

    pieces = jax.vmap(cut_strip)(starts)
    return lax.all_to_all(pieces, "py", split_axis=0, concat_axis=3, tiled=True)[0]


def from_strips(strip_values, starts, block_x, quarter_x):
    returned = lax.all_to_all(strip_values[None], "py", split_axis=3, concat_axis=0, tiled=True)
    pieces_count = returned.shape[0]
    strip_span = returned.shape[2]
    width_y = returned.shape[3]
    rows_total = quarter_x * lax.axis_size("px")
    canvas = jnp.zeros((returned.shape[1], rows_total + strip_span, width_y), jnp.float32)

    def place_strip(strip_index, canvas_now):
        first_row = starts[strip_index]
        current = lax.dynamic_slice_in_dim(canvas_now, first_row, strip_span, 1)
        piece = lax.dynamic_index_in_dim(returned, strip_index, 0, keepdims=False)
        return lax.dynamic_update_slice_in_dim(canvas_now, current + piece, first_row, 1)

    canvas = lax.fori_loop(0, pieces_count, place_strip, canvas)
    return lax.dynamic_slice_in_dim(canvas, 1 + block_x * quarter_x, quarter_x, 1)


def shards(source, coefficient, strip_rows):
    block_x = lax.axis_index("px")
    block_y = lax.axis_index("py")
    margin_width = max(PRE, POST)
    fine_int, fine_ext = prepare(coefficient, z_coupling, margin_width)
    mid_conduct = coarsen(coefficient)
    mid_int, mid_ext = prepare(mid_conduct, 4.0 * z_coupling, margin_width)
    low_conduct = coarsen(mid_conduct)
    starts = jnp.cumsum(strip_rows) - strip_rows
    quarter = low_conduct.shape[1]
    rows_total = quarter * lax.axis_size("px")
    most_rows = min(rows_total // 2 + quarter, rows_total - lax.axis_size("py") + 1)
    strip_conduct = to_strips(low_conduct, starts, most_rows)
    row_iota = jnp.arange(strip_conduct.shape[1], dtype=jnp.int32)
    own_rows = strip_rows[block_y]
    inside = jnp.broadcast_to(
        ((row_iota >= 1) & (row_iota <= own_rows))[None, :, None], strip_conduct.shape
    )
    inside_weight = inside.astype(jnp.float32)
    low_faces = face_arrays(strip_conduct, 16.0 * z_coupling)
    low_faces.append(invert(low_faces[6], inside))
    diag_total = jnp.sum(low_faces[6] * inside_weight)
    solution = jnp.zeros_like(source)
    for cycle_index in range(CYCLES):
        solution = smooth_level(solution, source, fine_int, PRE)
        mid_source = restrict(residual(solution, source, fine_int))
        middle = smooth_level(jnp.zeros_like(mid_source), mid_source, mid_int, PRE)
        low_source = restrict(residual(middle, mid_source, mid_int))
        strip_source = to_strips(low_source, starts, most_rows)
        strip_values = jnp.zeros_like(strip_source)
        for sweep_index in range(COARSE_SWEEPS):
            strip_values = relax_sweep(
                strip_values, pad_plain(strip_values), low_faces, strip_source
            )
        left_over = update(strip_values, pad_plain(strip_values), low_faces, strip_source)
        shift_strip = jnp.sum(left_over * inside_weight) / diag_total
        strip_values = strip_values + shift_strip * inside_weight
        correction = from_strips(strip_values, starts, block_x, quarter)
        middle = smooth_level(middle + prolong(correction), mid_source, mid_int, POST)
        solution = smooth_level(solution + prolong(middle), source, fine_int, POST)
    return solution


def solution(mesh):
    placed = (P(None, "px", "py"), P(None, "px", "py"), P())
    return jax.shard_map(
        shards, mesh=mesh, in_specs=placed, out_specs=P(None, "px", "py"), check_vma=False
    )
```

profile of v0, /device:TPU:1, one launch (start us, length us, event | category | flops | bytes accessed | tf_op | source)
XLA Modules:
  0.0 1130.3 jit_solution(14355110845164406667)
XLA Ops:
  20.3 23.6 %all_gather.9 = f32[8,128,32]{2,0,1:T(8,128)S(1)} all-gather(f32[8,8,32]{2,0,1:T(8,128)S(1)} %copy.411), channel_id=1, replica_groups=mesh['px'=16,'py'=16] {'px'}, dimensions={1}, use_global_device_ids=true | all-gather | bytes 139264 | tf_op jit(solution)/shard_map/all_gather | solution.py:111
  46.9 5.1 copy.412
  52.1 15.4 %all-to-all-start = ((f32[16,8,74,32]{2,3,1,0:T(8,128)}), f32[16,8,74,32]{2,3,1,0:T(8,128)S(1)}, u32[]{:S(2)}, u32[]{:S(2)}) async-start(f32[16,8,74,32]{2,3,1,0:T(8,128)} %copy.412), calls=%async_computation | async-start | bytes 4194304 | tf_op jit(solution)/shard_map/all_to_all | solution.py:118
  74.0 40.1 %collective-permute-done.22 = f32[1,8,18,1]{3,1,2,0:T(8,128)S(1)} collective-permute-done((f32[1,8,18,1]{3,1,2,0:T(8,128)S(1)}, f32[1,8,18,1]{3,1,2,0:T(8,128)S(1)}, u32[]{:S(2)}, u32[]{:S(2)}) %collective-permute-start.22) | collective-permute-done | bytes 608 | tf_op jit(solution)/shard_map/ppermute | solution.py:23
  182.4 5.6 collective-permute-done.19
  199.6 5.5 collective-permute-start.24
  240.3 21.0 %all_gather.10 = f32[8,128,32]{2,0,1:T(8,128)S(1)} all-gather(f32[8,8,32]{2,0,1:T(8,128)S(1)} %copy.421), channel_id=1, replica_groups=mesh['px'=16,'py'=16] {'px'}, dimensions={1}, use_global_device_ids=true | all-gather | bytes 139264 | tf_op jit(solution)/shard_map/all_gather | solution.py:111
  264.4 5.1 copy.422
  269.6 17.3 %all-to-all-start.1 = ((f32[16,8,74,32]{2,3,1,0:T(8,128)}), f32[16,8,74,32]{2,3,1,0:T(8,128)}, u32[]{:S(2)}, u32[]{:S(2)}) async-start(f32[16,8,74,32]{2,3,1,0:T(8,128)} %copy.422), calls=%async_computation.1 | async-start | bytes 4194304 | tf_op jit(solution)/shard_map/all_to_all | solution.py:118
  290.1 45.7 %all-to-all-done.1 = f32[16,8,74,32]{2,3,1,0:T(8,128)} async-done(((f32[16,8,74,32]{2,3,1,0:T(8,128)}), f32[16,8,74,32]{2,3,1,0:T(8,128)}, u32[]{:S(2)}, u32[]{:S(2)}) %all-to-all-start.1) | async-done | bytes 1212448 | tf_op jit(solution)/shard_map/all_to_all | solution.py:118
  339.1 14.3 %add_multiply_fusion.1 = (f32[8,74,512]{1,2,0:T(8,128)}, f32[8,74,512]{1,2,0:T(8,128)}, f32[8,74,512]{1,2,0:T(8,128)}, f32[8,74,512]{1,2,0:T(8,128)S(1)}, f32[8,...) fusion(f32[8,74,512]{1,2,0:T(8,128)S(1)} %bitcast.165, f32[7,74,512]{1,2,0:T(8,128)S(1)} %bitcast.151, ...), kind=kLoop, calls=%fused_computation.162 | loop fusion | flops 9699328 | bytes 13185130 | tf_op jit(solution)/shard_map/mul | solution.py:73
  353.4 5.1 fusion.262
  388.2 5.1 all-to-all-start.2
  393.3 49.1 %all-to-all-done.2 = f32[1,8,74,512]{2,1,0,3:T(8,128)} async-done(((f32[1,8,74,512]{2,1,0,3:T(8,128)}), f32[1,8,74,512]{2,1,0,3:T(8,128)}, u32[]{:S(2)}, u32[]{:S(2)}) %all-to-all-start.2) | async-done | bytes 1212448 | tf_op jit(solution)/shard_map/all_to_all | solution.py:122
  443.4 123.2 %while.26 = (s32[]{:T(128)}, f32[8,202,32]{2,1,0:T(8,128)}, s32[16]{0:T(128)S(1)}, f32[16,8,74,32]{2,1,3,0:T(8,128)}, s32[]{:T(128)}, /*index=5*/s32[]{:T(128)}, s32[]{:T(128)}) while((s32[]{:T(128)}, f32[8,202,32]{2,1,0:T(8,128)}, s32[16]{0:T(128)S(1)}, f32[16,8,74,32]{2,1,3,0:T(8,128)}, s32[]{:T(128)}, /*index=5*/s32[]{:T(128)}, ...), condition=%wide.region_8.9_spmd, body=%wide.region_7.8_spmd.sunk | while | flops 18949 | bytes 682119 | solution.py:135
  606.0 5.7 collective-permute-start.40
  699.0 5.2 collective-permute-done.59
  754.0 21.8 %all_gather.11 = f32[8,128,32]{2,0,1:T(8,128)S(1)} all-gather(f32[8,8,32]{2,0,1:T(8,128)S(1)} %copy.456), channel_id=1, replica_groups=mesh['px'=16,'py'=16] {'px'}, dimensions={1}, use_global_device_ids=true | all-gather | bytes 139264 | tf_op jit(solution)/shard_map/all_gather | solution.py:111
  778.9 5.1 copy.457
  784.0 67.0 %all_to_all.81 = f32[16,8,74,32]{2,3,1,0:T(8,128)S(1)} all-to-all(f32[16,8,74,32]{2,3,1,0:T(8,128)} %copy.457), channel_id=1, replica_groups=mesh['px'=16,'py'=16] {'py'}, dimensions={0} | all-to-all | bytes 2424832 | tf_op jit(solution)/shard_map/all_to_all | solution.py:118
  853.3 5.1 add_multiply_fusion
  893.9 48.2 %all-to-all-done.4 = f32[1,8,74,512]{2,1,0,3:T(8,128)S(1)} async-done(((f32[1,8,74,512]{2,1,0,3:T(8,128)}), f32[1,8,74,512]{2,1,0,3:T(8,128)S(1)}, u32[]{:S(2)}, u32[]{:S(2)}) %all-to-all-start.4) | async-done | bytes 1212448 | tf_op jit(solution)/shard_map/all_to_all | solution.py:122
  943.6 113.2 %while.27 = (s32[]{:T(128)}, f32[8,202,32]{2,1,0:T(8,128)S(1)}, s32[16]{0:T(128)S(1)}, f32[16,8,74,32]{2,1,3,0:T(8,128)}, s32[]{:T(128)}, /*index=5*/s32[]{:T(128)}, s32[]{:T(128)}) while((s32[]{:T(128)}, f32[8,202,32]{2,1,0:T(8,128)S(1)}, s32[16]{0:T(128)S(1)}, f32[16,8,74,32]{2,1,3,0:T(8,128)}, s32[]{:T(128)}, /*index=5*/s32[]{:T(128)}, ...), condition=%wide.region_13.14_spmd, body=%wide.region_12.13_spmd.sunk | while | flops 18949 | bytes 682119 | solution.py:135
  1090.3 5.2 collective-permute-start.76
  (711 shorter events, 645.2 us)
Async XLA Ops:
  0.0 120.1 %collective-permute-start.4 = (f32[1,8,1,128]{3,1,2,0:T(8,128)S(1)}, f32[1,8,1,128]{3,1,2,0:T(8,128)S(1)}, u32[]{:S(2)}, u32[]{:S(2)}) collective-permute-start(f32[1,8,1,128]{3,1,2,0:T(8,128)S(1)} %broadcast.262), channel_id=1, source_target_pairs={{0,16},{16,32},{32,48},{48,64},{64,80},{80,96},{96,112},{112,128},... | collective-permute-start | bytes 12296 | tf_op jit(solution)/shard_map/ppermute | solution.py:23
  3.9 117.5 %collective-permute-start.5 = (f32[1,8,1,128]{3,1,2,0:T(8,128)S(1)}, f32[1,8,1,128]{3,1,2,0:T(8,128)S(1)}, u32[]{:S(2)}, u32[]{:S(2)}) collective-permute-start(f32[1,8,1,128]{3,1,2,0:T(8,128)S(1)} %broadcast.262), channel_id=1, source_target_pairs={{16,0},{32,16},{48,32},{64,48},{80,64},{96,80},{112,96},{128,112},... | collective-permute-start | bytes 12296 | tf_op jit(solution)/shard_map/ppermute | solution.py:24
  5.3 62.2 %collective-permute-start.20 = (f32[1,8,1,64]{3,1,2,0:T(8,128)S(1)}, f32[1,8,1,64]{3,1,2,0:T(8,128)S(1)}, u32[]{:S(2)}, u32[]{:S(2)}) collective-permute-start(f32[1,8,1,64]{3,1,2,0:T(8,128)S(1)} %broadcast.266), channel_id=1, source_target_pairs={{0,16},{16,32},{32,48},{48,64},{64,80},{80,96},{96,112},{112,128},... | collective-permute-start | bytes 6152 | tf_op jit(solution)/shard_map/ppermute | solution.py:23
  9.2 58.2 %collective-permute-start.21 = (f32[1,8,1,64]{3,1,2,0:T(8,128)S(1)}, f32[1,8,1,64]{3,1,2,0:T(8,128)S(1)}, u32[]{:S(2)}, u32[]{:S(2)}) collective-permute-start(f32[1,8,1,64]{3,1,2,0:T(8,128)S(1)} %broadcast.266), channel_id=1, source_target_pairs={{16,0},{32,16},{48,32},{64,48},{80,64},{96,80},{112,96},{128,112},... | collective-permute-start | bytes 6152 | tf_op jit(solution)/shard_map/ppermute | solution.py:24
  11.6 126.8 %collective-permute-start = (f32[1,8,2,128]{3,1,2,0:T(8,128)S(1)}, f32[1,8,2,128]{3,1,2,0:T(8,128)S(1)}, u32[]{:S(2)}, u32[]{:S(2)}) collective-permute-start(f32[1,8,2,128]{3,1,2,0:T(8,128)S(1)} %get-tuple-element.341), channel_id=1, source_target_pairs={{0,16},{16,32},{32,48},{48,64},{64,80},{80,96},{96,112},{112,128},... | collective-permute-start | bytes 24584 | tf_op jit(solution)/shard_map/ppermute | solution.py:23
  52.1 217.5 %all-to-all-start = ((f32[16,8,74,32]{2,3,1,0:T(8,128)}), f32[16,8,74,32]{2,3,1,0:T(8,128)S(1)}, u32[]{:S(2)}, u32[]{:S(2)}) async-start(f32[16,8,74,32]{2,3,1,0:T(8,128)} %copy.412), calls=%async_computation | async-start | bytes 4194304 | tf_op jit(solution)/shard_map/all_to_all | solution.py:118
  67.6 46.5 %collective-permute-start.22 = (f32[1,8,18,1]{3,1,2,0:T(8,128)S(1)}, f32[1,8,18,1]{3,1,2,0:T(8,128)S(1)}, u32[]{:S(2)}, u32[]{:S(2)}) collective-permute-start(f32[1,8,18,1]{3,1,2,0:T(8,128)S(1)} %get-tuple-element.363), channel_id=1, source_target_pairs={{0,1},{1,2},{2,3},{3,4},{4,5},{5,6},{6,7},{7,8},{8,9},{9,10},{10,1... | collective-permute-start | bytes 1736 | tf_op jit(solution)/shard_map/ppermute | solution.py:23
  71.1 45.0 %collective-permute-start.23 = (f32[1,8,18,1]{3,1,2,0:T(8,128)S(1)}, f32[1,8,18,1]{3,1,2,0:T(8,128)S(1)}, u32[]{:S(2)}, u32[]{:S(2)}) collective-permute-start(f32[1,8,18,1]{3,1,2,0:T(8,128)S(1)} %get-tuple-element.364), channel_id=1, source_target_pairs={{1,0},{2,1},{3,2},{4,3},{5,4},{6,5},{7,6},{8,7},{9,8},{10,9},{11,1... | collective-permute-start | bytes 1736 | tf_op jit(solution)/shard_map/ppermute | solution.py:24
  114.1 24.3 %collective-permute-start.1 = (f32[1,8,2,128]{3,1,2,0:T(8,128)S(1)}, f32[1,8,2,128]{3,1,2,0:T(8,128)S(1)}, u32[]{:S(2)}, u32[]{:S(2)}) collective-permute-start(f32[1,8,2,128]{3,1,2,0:T(8,128)S(1)} %get-tuple-element.342), channel_id=1, source_target_pairs={{16,0},{32,16},{48,32},{64,48},{80,64},{96,80},{112,96},{128,112},... | collective-permute-start | bytes 24584 | tf_op jit(solution)/shard_map/ppermute | solution.py:24
  116.2 10.5 collective-permute-start.12
  120.1 8.5 collective-permute-start.13
  121.7 10.8 collective-permute-start.6
  126.6 7.8 collective-permute-start.7
  140.5 6.6 collective-permute-start.3
  160.6 6.6 collective-permute-start.11
  180.2 7.9 collective-permute-start.19
  199.6 6.8 collective-permute-start.24
  230.6 6.7 collective-permute-start.31
  269.6 66.2 %all-to-all-start.1 = ((f32[16,8,74,32]{2,3,1,0:T(8,128)}), f32[16,8,74,32]{2,3,1,0:T(8,128)}, u32[]{:S(2)}, u32[]{:S(2)}) async-start(f32[16,8,74,32]{2,3,1,0:T(8,128)} %copy.422), calls=%async_computation.1 | async-start | bytes 4194304 | tf_op jit(solution)/shard_map/all_to_all | solution.py:118
  388.2 54.2 %all-to-all-start.2 = ((f32[1,8,74,512]{2,1,0,3:T(8,128)}), f32[1,8,74,512]{2,1,0,3:T(8,128)}, u32[]{:S(2)}, u32[]{:S(2)}) async-start(f32[1,8,74,512]{2,1,0,3:T(8,128)} %copy.424), calls=%async_computation.2 | async-start | bytes 4194304 | tf_op jit(solution)/shard_map/all_to_all | solution.py:122
  606.0 7.0 collective-permute-start.40
  677.2 7.1 collective-permute-start.55
  696.7 7.6 collective-permute-start.59
  890.3 51.9 %all-to-all-start.4 = ((f32[1,8,74,512]{2,1,0,3:T(8,128)}), f32[1,8,74,512]{2,1,0,3:T(8,128)S(1)}, u32[]{:S(2)}, u32[]{:S(2)}) async-start(f32[1,8,74,512]{2,1,0,3:T(8,128)} %copy.459), calls=%async_computation.4 | async-start | bytes 4194304 | tf_op jit(solution)/shard_map/all_to_all | solution.py:122
  (132 other events, 1992.7 us)
where the time goes:
time: 1150 us; the launch traced here: 1130 us
  waiting for transfers between devices  323 us (28%)
  starting transfers between devices  256 us (22%)
  local copies, waits for them, and re-layouts  240 us (21%)
  blocking collectives  133 us (12%)
  other arithmetic  114 us (10%)
  loops' own time  57.7 us (5%)
    ppermute x42, starting transfers between devices, extended(): before = lax.ppermute(last, axis, up)  146 us
    ppermute x42, waiting for transfers between devices, extended(): after = lax.ppermute(initial, axis, down)  137 us
    dynamic_update_slice x32, local copies, waits for them, and re-layouts, place_strip(): lax.dynamic_update_slice_in_dim(canvas_now, current + piece, first_row, 1)  107 us
    all_to_all x2, waiting for transfers between devices, from_strips(): lax.all_to_all(strip_values[None], 'py', split_axis=3, concat_axis=0, til...  97.3 us
    ppermute x42, starting transfers between devices, extended(): after = lax.ppermute(initial, axis, down)  68.6 us
    all_to_all x1, blocking collectives, to_strips(): lax.all_to_all(pieces, 'py', split_axis=0, concat_axis=3, tiled=True)[0]  67 us
    all_gather x3, blocking collectives, to_strips(): gathered = lax.all_gather(level_values, 'px', axis=1, tiled=True)  66.4 us
    another operation x2, loops' own time, from_strips(): canvas = lax.fori_loop(0, pieces_count, place_strip, canvas)  57.7 us
  transfers between devices with their start and end apart: 88, of which 48 were waited for; matrix products, arithmetic and copies ran while one was open for 4% of the time, Pallas kernels for 0%

commit v1 on v0

v1 whole, which is shorter than its diff:
```python
import jax
import jax.numpy as jnp
from jax import lax
from jax.experimental import pallas as pl
from jax.experimental.pallas import tpu as pltpu
from jax.sharding import PartitionSpec as P

CYCLES = 2
COARSE_SWEEPS = 6
relaxation = 0.8
z_coupling = 0.25

MESH = pl.DeviceIdType.MESH

NZ = 8
ROWS = 32
LANES = 128
EDGE = 16
HALO = 12
FINE = ROWS + 2 * HALO
MID = FINE // 2
OWN2 = ROWS // 4
LOW = 3 * OWN2
SHIFTED = OWN2 + 8


def lanes_of(rows):
    return lax.broadcasted_iota(jnp.int32, (rows, NZ, LANES), 2)


def layers_of(rows):
    return lax.broadcasted_iota(jnp.int32, (rows, NZ, LANES), 1)


def beside_lanes(pair, step, tiles):
    lane = lanes_of(pair[0].shape[0])
    back = [pltpu.roll(part, step, 2) for part in pair]
    ahead = [pltpu.roll(part, LANES - step, 2) for part in pair]
    before, after = lane < step, lane >= LANES - step
    south = [jnp.where(before, back[1 - t], back[t]) for t in tiles]
    north = [jnp.where(after, ahead[1 - t], ahead[t]) for t in tiles]
    return south, north


def weighted(values, weights, row, rows, step, tiles=(0, 1)):
    pair = [values[t, pl.ds(row + 1, rows)] for t in (0, 1)]
    south, north = beside_lanes(pair, step, tiles)
    totals = []
    for at, t in enumerate(tiles):
        here = pl.ds(row, rows)
        total = weights[0, t, here] * values[t, pl.ds(row, rows)]
        total += weights[1, t, here] * values[t, pl.ds(row + 2, rows)]
        total += weights[2, t, here] * south[at]
        total += weights[3, t, here] * north[at]
        total += weights[4, t, here] * pltpu.roll(pair[t], 1, 1)
        total += weights[5, t, here] * pltpu.roll(pair[t], NZ - 1, 1)
        totals.append(total)
    return [pair[t] for t in tiles], totals


def loop(count, body):
    def step(index, nothing):
        body(index)
        return nothing

    lax.fori_loop(0, count, step, 0)


def sweep(values, new, weights, right, first, count, rows, step):
    def body(index):
        row = first + index * rows
        old, total = weighted(values, weights, row, rows, step)
        for t in (0, 1):
            base = (1.0 - relaxation) * old[t] + total[t]
            if right is not None:
                base += right[t, pl.ds(row, rows)]
            new[t, pl.ds(row + 1, rows)] = base

    loop(count, body)


def make_weights(conduct, weights, row, rows, step, z_factor, keep=None):
    pair = [conduct[t, pl.ds(row + 1, rows)] for t in (0, 1)]
    south, north = beside_lanes(pair, step, (0, 1))
    layer = layers_of(rows)
    inverses, diagonals = [], []
    for t in (0, 1):
        own = pair[t]
        faces = [
            0.5 * (own + conduct[t, pl.ds(row, rows)]),
            0.5 * (own + conduct[t, pl.ds(row + 2, rows)]),
            0.5 * (own + south[t]),
            0.5 * (own + north[t]),
            jnp.where(layer > 0, (0.5 * z_factor) * (own + pltpu.roll(own, 1, 1)), 0.0),
            jnp.where(layer < NZ - 1, (0.5 * z_factor) * (own + pltpu.roll(own, NZ - 1, 1)), 0.0),
        ]
        diagonal = faces[0] + faces[1] + faces[2] + faces[3] + faces[4] + faces[5]
        inside = own > 0.0
        inverse = jnp.where(inside, relaxation / jnp.where(inside, diagonal, 1.0), 0.0)
        if keep is not None:
            faces[0] = faces[0] * keep[pl.ds(row, rows)]
            faces[1] = faces[1] * keep[pl.ds(row + 1, rows)]
        for side in range(6):
            weights[side, t, pl.ds(row, rows)] = inverse * faces[side]
        inverses.append(inverse)
        diagonals.append(diagonal)
    return inverses, diagonals


def pair_rows(values):
    rows = values.shape[0]
    return jnp.sum(values.reshape(rows // 2, 2, NZ, LANES), axis=1)


def pair_lanes(values, step):
    lane = lanes_of(values.shape[0])
    other = jnp.where(
        (lane // step) % 2 == 0, pltpu.roll(values, LANES - step, 2), pltpu.roll(values, step, 2)
    )
    return values + other


def twice_rows(values):
    rows = values.shape[0]
    wide = jnp.broadcast_to(values[:, None], (rows, 2, NZ, LANES))
    return wide.reshape(2 * rows, NZ, LANES)


def roll_lanes(tile, amount):
    amount = amount % LANES
    return tile if amount == 0 else pltpu.roll(tile, amount, 1)


def pack_edges(block, group, right_side):
    lane = lax.broadcasted_iota(jnp.int32, (NZ, LANES), 1)
    packed = None
    for j in range(8):
        moved = roll_lanes(block[8 * group + j], EDGE * j + (EDGE if right_side else 0))
        packed = moved if packed is None else jnp.where(lane // EDGE == j, moved, packed)
    return packed


def unpack_edges(left, right, j):
    lane = lax.broadcasted_iota(jnp.int32, (NZ, LANES), 1)
    from_right = roll_lanes(right, -EDGE * j)
    from_left = roll_lanes(left, -EDGE * (j + 1))
    return jnp.where(lane < EDGE, from_right, jnp.where(lane >= LANES - EDGE, from_left, 0.0))


def pack_quads(rows):
    lane = lax.broadcasted_iota(jnp.int32, (NZ, LANES), 1) % 4
    out = rows[3]
    for m in range(3):
        out = jnp.where(lane == m, rows[m], out)
    return out


def unpack_quad(packed, m):
    lane = lax.broadcasted_iota(jnp.int32, (NZ, LANES), 1) % 4
    one = roll_lanes(jnp.where(lane == m, packed, 0.0), -m)
    one = one + roll_lanes(one, 1)
    return one + roll_lanes(one, 2)


class Exchange:
    def __init__(self, depth, extra):
        self.depth, self.extra = depth, extra
        sizes = [depth + extra] * 2 + [4 + extra] * 2 + [2 + extra] * 4
        self.at = [sum(sizes[:i]) for i in range(9)]

    def stage_rows(self, send, block):
        send[0:self.depth] = block[ROWS - self.depth:ROWS]
        send[self.depth + self.extra:2 * self.depth + self.extra] = block[0:self.depth]

    def stage_edges(self, edges, block):
        for side in (0, 1):
            for group in range(4):
                at = group if group < 2 else group + self.extra
                edges[side, at] = pack_edges(block, group, side == 1)

    def stage_extra(self, send, edges, at, tile):
        send[self.depth + at] = tile
        for side in (0, 1):
            edges[side, 2 + at] = tile

    def start(self, send, edges, got, send_sem, got_sem, near):
        n, x, at = self.depth, self.extra, self.at
        top, bottom = pl.ds(0, 2 + x), pl.ds(2, 2 + x)
        moves = [
            (send.at[pl.ds(0, n + x)], 0, (1, 0)),
            (send.at[pl.ds(n, n + x)], 1, (-1, 0)),
            (edges.at[1], 2, (0, 1)),
            (edges.at[0], 3, (0, -1)),
            (edges.at[1, bottom], 4, (1, 1)),
            (edges.at[0, bottom], 5, (1, -1)),
            (edges.at[1, top], 6, (-1, 1)),
            (edges.at[0, top], 7, (-1, -1)),
        ]
        for source, slot, way in moves:
            pltpu.make_async_remote_copy(
                src_ref=source,
                dst_ref=got.at[pl.ds(at[slot], at[slot + 1] - at[slot])],
                send_sem=send_sem,
                recv_sem=got_sem,
                device_id=near(*way),
                device_id_type=MESH,
            ).start()

    def unpack(self, got, put_rows, put_beside):
        n, x, at = self.depth, self.extra, self.at
        put_rows(HALO - n, n, got[at[0]:at[0] + n])
        put_rows(HALO + ROWS, n, got[at[1] + x:at[1] + x + n])
        for i in range(FINE):
            if i < HALO:
                source = ROWS - HALO + i
                offset = at[4] + x - 2, at[5] + x - 2
            elif i < HALO + ROWS:
                source = i - HALO
                shift = x if source >= ROWS // 2 else 0
                offset = at[2] + shift, at[3] + shift
            else:
                source = i - HALO - ROWS
                offset = at[6], at[7]
            group, j = divmod(source, 8)
            put_beside(i, unpack_edges(got[offset[0] + group], got[offset[1] + group], j))

    def extras(self, got, a, b, q):
        n, x, at = self.depth, self.extra, self.at
        where = {
            (-1, 0): at[0] + n,
            (1, 0): at[1],
            (0, -1): at[2] + 2,
            (0, 1): at[3] + 2,
            (-1, -1): at[4],
            (-1, 1): at[5],
            (1, -1): at[6] + 2,
            (1, 1): at[7] + 2,
        }
        return got[where[(a, b)] + q]


AROUND = [(a, b) for a in (-1, 0, 1) for b in (-1, 0, 1) if (a, b) != (0, 0)]
FOR_K = Exchange(HALO, 2)
FOR_F = Exchange(HALO - 2, 0)
FOR_S = Exchange(HALO - 1, 0)


def kernel(strip_ref, source_ref, coefficient_ref, out_ref,
           k_own, f_own, s_own, k_send, f_send, s_send, k_edge, f_edge, s_edge,
           k_got, f_got, s_got,
           k0, c0, g0, d0, va, vb, k1, c1, i1, g1, d1, ua, ub, k2, c2, i2, g2, ea, eb,
           weight, diag_sum, keep, shifts, pick, l_own, l_send, l_got, one_send, one_got, two_send,
           two_got, sems):
    px, py = lax.axis_index("px"), lax.axis_index("py")
    size_x, size_y = lax.axis_size("px"), lax.axis_size("py")
    strips = strip_ref.shape[0]

    def near(a, b):
        return (lax.rem(px + a + size_x, size_x), lax.rem(py + b + size_y, size_y))

    peers = [(0, b) for b in range(1, size_y)] + [(a, 0) for a in range(1, size_x)]
    peers += [way for way in AROUND if way[0] and way[1]]
    barrier = pltpu.get_barrier_semaphore()
    for way in peers:
        pl.semaphore_signal(barrier, inc=1, device_id=near(*way), device_id_type=MESH)

    def arrived(buffer, sem):
        pltpu.make_async_copy(buffer, buffer, sem).wait()

    for r in range(ROWS):
        k_own[r] = coefficient_ref[pl.ds(r, NZ, stride=ROWS), :]
        f_own[r] = source_ref[pl.ds(r, NZ, stride=ROWS), :]

    zero = jnp.zeros((NZ, LANES), jnp.float32)
    FOR_K.stage_rows(k_send, k_own)
    FOR_K.stage_edges(k_edge, k_own)
    for q in (0, 1):
        mids = 0.25 * pair_lanes(pair_rows(k_own[16 * q:16 * q + 16]), 1)
        lows = 0.25 * pair_lanes(pair_rows(mids), 2)
        k2[0, 1 + OWN2 + 4 * q:1 + OWN2 + 4 * q + 4] = lows
        FOR_K.stage_extra(k_send, k_edge, q, pack_quads([lows[m] for m in range(4)]))
    FOR_F.stage_rows(f_send, f_own)
    FOR_F.stage_edges(f_edge, f_own)
    pl.semaphore_wait(barrier, len(peers))
    FOR_K.start(k_send, k_edge, k_got, sems.at[0], sems.at[1], near)
    FOR_F.start(f_send, f_edge, f_got, sems.at[2], sems.at[3], near)

    ends, total = [], jnp.int32(0)
    for c in range(strips):
        total = total + strip_ref[c]
        ends.append(total)
    sub = lax.broadcasted_iota(jnp.int32, (8, LANES), 0)
    lane = lax.broadcasted_iota(jnp.int32, (8, LANES), 1)

    def strip_of(rows):
        found = jnp.zeros_like(rows)
        for end in ends:
            found = found + jnp.where(rows >= end, 1, 0)
        return found

    for tile in range(4):
        rows = OWN2 * px - OWN2 + 8 * tile + sub
        kept = jnp.ones((8, LANES), jnp.float32)
        for end in ends:
            kept = jnp.where(rows == end, 0.0, kept)
        for i in range(8 if tile < 3 else 1):
            keep[8 * tile + i] = jnp.broadcast_to(kept[i:i + 1], (NZ, LANES))
    lane_strip = strip_of(lane)
    for tile in (0, 1):
        rows = jnp.clip(OWN2 * px - 4 + 8 * tile + sub, 0, OWN2 * size_x - 1)
        pick[tile] = jnp.where(strip_of(rows) == lane_strip, 1.0, 0.0)

    for ref, end in ((k0, FINE), (va, FINE), (vb, FINE), (k1, MID), (ua, MID), (ub, MID),
                     (k2, LOW), (ea, LOW), (eb, LOW)):
        for t in (0, 1):
            ref[t, 0] = zero
            ref[t, end + 1] = zero

    wide_lane = lax.broadcasted_iota(jnp.int32, (NZ, LANES), 1)
    inner_x = (px > 0, px < size_x - 1)
    inner_y = jnp.where(
        wide_lane < LANES // 2,
        jnp.where(py < size_y - 1, 1.0, 0.0), jnp.where(py > 0, 1.0, 0.0)
    )
    row_in = [jnp.where(flag, 1.0, 0.0) for flag in inner_x]

    def put_k_rows(first, rows, values):
        k0[0, 1 + first:1 + first + rows] = values * row_in[0 if first < HALO else 1]

    def put_k_beside(i, tile):
        tile = tile * inner_y
        if i < HALO or i >= HALO + ROWS:
            tile = tile * row_in[0 if i < HALO else 1]
        k0[1, 1 + i] = tile

    k0[0, 1 + HALO:1 + HALO + ROWS] = k_own[...]
    arrived(k_got, sems.at[1])
    FOR_K.unpack(k_got, put_k_rows, put_k_beside)

    def low_tiles(get, put):
        for at, a in enumerate((-1, 0, 1)):
            for q in (0, 1):
                if a != 0:
                    tile = get(a, 0, q)
                    for m in range(4):
                        put(0, OWN2 * at + 4 * q + m, a, unpack_quad(tile, m))
                tile = jnp.where(wide_lane < LANES // 2, get(a, 1, q), get(a, -1, q))
                for m in range(4):
                    put(1, OWN2 * at + 4 * q + m, a, unpack_quad(tile, m))

    def put_k2(t, row, a, tile):
        if t == 1:
            tile = tile * inner_y
        if a != 0:
            tile = tile * row_in[0 if a < 0 else 1]
        k2[t, 1 + row] = tile

    low_tiles(lambda a, b, q: FOR_K.extras(k_got, a, b, q), put_k2)

    def weights_2(index):
        row = index * 8
        inverse, diagonal = make_weights(k2, c2, row, 8, 4, 16.0 * z_coupling, keep)
        for t in (0, 1):
            i2[t, pl.ds(row, 8)] = inverse[t]
            ea[t, pl.ds(row + 1, 8)] = jnp.where(k2[t, pl.ds(row + 1, 8)] > 0.0, 1.0, 0.0)

        @pl.when(index == 1)
        def _():
            diag_sum[...] = jnp.sum(diagonal[0], axis=1)

    loop(3, weights_2)

    def weights_0(index):
        row = index * 8
        inverse, diagonal = make_weights(k0, c0, row, 8, 1, z_coupling)
        for t in (0, 1):
            g0[t, pl.ds(row, 8)] = inverse[t]
            d0[t, pl.ds(row, 8)] = (1.0 / relaxation) * diagonal[t]
            half = pl.multiple_of(index * 4, 4)
            k1[t, pl.ds(half + 1, 4)] = 0.25 * pair_lanes(
                pair_rows(k0[t, pl.ds(row + 1, 8)]), 1)

    loop(FINE // 8, weights_0)

    def weights_1(index):
        row = index * 7
        inverse, diagonal = make_weights(k1, c1, row, 7, 2, 4.0 * z_coupling)
        for t in (0, 1):
            i1[t, pl.ds(row, 7)] = inverse[t]
            d1[t, pl.ds(row, 7)] = (1.0 / relaxation) * diagonal[t]

    loop(MID // 7, weights_1)

    for turn in range(COARSE_SWEEPS):
        here, there = (ea, eb) if turn % 2 == 0 else (eb, ea)
        sweep(here, there, c2, None, 0, 3, 8, 4)
    done = ea if COARSE_SWEEPS % 2 == 0 else eb
    weight[...] = done[0, 1 + OWN2:1 + 2 * OWN2]

    va[0, 1 + HALO:1 + HALO + ROWS] = f_own[...]

    def put_f_rows(first, rows, values):
        va[0, 1 + first:1 + first + rows] = values

    def put_f_beside(i, tile):
        va[1, 1 + i] = tile

    for i in (0, 1, FINE - 2, FINE - 1):
        va[0, 1 + i] = zero
    arrived(f_got, sems.at[3])
    FOR_F.unpack(f_got, put_f_rows, put_f_beside)

    def first_sweep(index):
        row = index * 8
        for t in (0, 1):
            start = g0[t, pl.ds(row, 8)] * va[t, pl.ds(row + 1, 8)]
            g0[t, pl.ds(row, 8)] = start
            va[t, pl.ds(row + 1, 8)] = start

    loop(FINE // 8, first_sweep)

    dens = None
    used = 4
    for cycle in range(CYCLES):
        if cycle > 0:
            sweep(va, vb, c0, g0, 0, FINE // 8, 8, 1)
            sweep(vb, va, c0, g0, 0, FINE // 8, 8, 1)
            fine, spare = va, vb
        else:
            sweep(va, vb, c0, g0, 0, FINE // 8, 8, 1)
            fine, spare = vb, va

        def down(index, fine=fine):
            row = index * 8
            old, total = weighted(fine, c0, row, 8, 1)
            for t in (0, 1):
                here = pl.ds(row, 8)
                rest = d0[t, here] * (g0[t, here] - relaxation * old[t] + total[t])
                half = pl.multiple_of(index * 4, 4)
                start = i1[t, pl.ds(half, 4)] * pair_lanes(pair_rows(rest), 1)
                g1[t, pl.ds(half, 4)] = start
                ua[t, pl.ds(half + 1, 4)] = start

        loop(FINE // 8, down)
        sweep(ua, ub, c1, g1, 0, MID // 7, 7, 2)

        def lower(index):
            row = HALO // 2 + index * 8
            old, total = weighted(ub, c1, row, 8, 2, (0,))
            here = pl.ds(row, 8)
            rest = d1[0, here] * (g1[0, here] - relaxation * old[0] + total[0])
            l_own[pl.ds(index * 4, 4)] = pair_lanes(pair_rows(rest), 2)

        loop(2, lower)

        sums = jnp.sum(weight[...] * l_own[...], axis=1)
        if cycle == 0:
            sums = jnp.where(lane % 4 == 0, sums, jnp.where(lane % 4 == 1, diag_sum[...], 0.0))
        one_send[cycle] = sums
        wide = 2 if cycle == 0 else 1

        def spread(source, got, sem, ways):
            for slot, way in enumerate(ways):
                pltpu.make_async_remote_copy(
                    src_ref=source,
                    dst_ref=got.at[slot],
                    send_sem=sems.at[sem],
                    recv_sem=sems.at[sem + 1],
                    device_id=near(*way),
                    device_id_type=MESH,
                ).start()

        one_in = one_got.at[cycle]
        spread(one_send.at[cycle], one_in, used, [(0, b) for b in range(1, size_y)])
        for q in (0, 1):
            l_send[cycle, q] = pack_quads([l_own[4 * q + m] for m in range(4)])
        low_in = l_got.at[cycle]
        spread(l_send.at[cycle], low_in, used + 2, [(-a, -b) for a, b in AROUND])
        arrived(one_in, sems.at[used + 1])
        sums = one_send[cycle] + jnp.sum(one_got[cycle], axis=0)
        mine = lane == OWN2 * px + sub
        for part in range(wide):
            column = jnp.sum(jnp.where(lane % 4 == part, sums, 0.0), axis=1, keepdims=True)
            two_send[cycle, part] = jnp.where(mine, column, 0.0)
        two_in = two_got.at[cycle, :, pl.ds(0, wide)] if wide == 1 else two_got.at[cycle]
        two_out = two_send.at[cycle, pl.ds(0, wide)]
        spread(two_out, two_in, used + 4, [(a, 0) for a in range(1, size_x)])

        arrived(low_in, sems.at[used + 3])

        def put_low(t, row, a, tile):
            start = i2[t, row] * tile
            g2[t, row] = start
            ea[t, 1 + row] = start

        low_tiles(lambda a, b, q: l_got[cycle, AROUND.index((a, b)), q], put_low)
        for r in range(OWN2):
            put_low(0, OWN2 + r, 0, l_own[r])
        for turn in range(COARSE_SWEEPS - 1):
            here, there = (ea, eb) if turn % 2 == 0 else (eb, ea)
            sweep(here, there, c2, g2, 0, 3, 8, 4)
        low = eb if COARSE_SWEEPS % 2 == 0 else ea

        arrived(two_in, sems.at[used + 5])
        parts = []
        for part in range(wide):
            both = two_send[cycle, part] + jnp.sum(two_got[cycle, :, part], axis=0)
            row_sums = jnp.broadcast_to(jnp.sum(both, axis=0, keepdims=True), (8, LANES))
            parts.append([jnp.sum(pick[tile] * row_sums, axis=1, keepdims=True) for tile in (0, 1)])
        if cycle == 0:
            dens = parts[1]
        for tile in (0, 1):
            shift = jnp.broadcast_to(parts[0][tile] / dens[tile], (8, LANES))
            for i in range(8):
                shifts[8 * tile + i] = jnp.broadcast_to(shift[i:i + 1], (NZ, LANES))

        def up_1(index):
            row = 2 + index * 8
            from_low = HALO // 4 + index * 4 + 3
            for t in (0, 1):
                here = pl.ds(from_low + 1, 4)
                inside = k2[t, here] > 0.0
                moved = jnp.where(inside, shifts[pl.ds(index * 4 + 2, 4)], 0.0)
                ua[t, pl.ds(row + 1, 8)] = ub[t, pl.ds(row + 1, 8)] + twice_rows(
                    low[t, here] + moved)

        loop(3, up_1)
        sweep(ua, ub, c1, g1, 2, 3, 8, 2)
        sweep(ub, ua, c1, g1, 2, 3, 8, 2)

        def up_0(index, fine=fine, spare=spare):
            row = 8 + index * 8
            for t in (0, 1):
                here = pl.ds(row + 1, 8)
                spare[t, here] = fine[t, here] + twice_rows(ua[t, pl.ds(4 + index * 4 + 1, 4)])

        loop(5, up_0)
        sweep(spare, fine, c0, g0, 8, 5, 8, 1)

        def last(index, fine=fine):
            row = HALO + index * 8
            old, total = weighted(fine, c0, row, 8, 1, (0,))
            done = g0[0, pl.ds(row, 8)] + (1.0 - relaxation) * old[0] + total[0]
            s_own[pl.ds(index * 8, 8)] = done

        loop(ROWS // 8, last)
        used += 6

        if cycle < CYCLES - 1:
            FOR_S.stage_rows(s_send, s_own)
            FOR_S.stage_edges(s_edge, s_own)
            FOR_S.start(s_send, s_edge, s_got, sems.at[used], sems.at[used + 1], near)
            va[0, 1 + HALO:1 + HALO + ROWS] = s_own[...]
            va[0, 1] = zero
            va[0, FINE] = zero

            def put_s_rows(first, rows, values):
                inside = k0[0, 1 + first:1 + first + rows] > 0.0
                va[0, 1 + first:1 + first + rows] = jnp.where(inside, values, 0.0)

            def put_s_beside(i, tile):
                va[1, 1 + i] = jnp.where(k0[1, 1 + i] > 0.0, tile, 0.0)

            arrived(s_got, sems.at[used + 1])
            FOR_S.unpack(s_got, put_s_rows, put_s_beside)
            used += 2

    for r in range(ROWS):
        out_ref[pl.ds(r, NZ, stride=ROWS), :] = s_own[r]

    arrived(k_got, sems.at[0])
    arrived(f_got, sems.at[2])
    arrived(one_got.at[0], sems.at[4])
    arrived(l_got.at[0], sems.at[6])
    arrived(two_got.at[0], sems.at[8])
    arrived(s_got, sems.at[10])
    arrived(one_got.at[1], sems.at[12])
    arrived(l_got.at[1], sems.at[14])
    arrived(two_got.at[1, :, pl.ds(0, 1)], sems.at[16])


def vmem(*shape):
    return pltpu.VMEM(shape + (NZ, LANES), jnp.float32)


def shards(source, coefficient, strip_rows):
    size_x, size_y = lax.axis_size("px"), lax.axis_size("py")
    flat = (NZ * ROWS, LANES)
    scratch = [vmem(ROWS), vmem(ROWS), vmem(ROWS)]
    scratch += [vmem(2 * e.depth + e.extra) for e in (FOR_K, FOR_F, FOR_S)]
    scratch += [vmem(2, 4 + e.extra) for e in (FOR_K, FOR_F, FOR_S)]
    scratch += [vmem(e.at[8]) for e in (FOR_K, FOR_F, FOR_S)]
    scratch += [vmem(2, FINE + 2), vmem(6, 2, FINE), vmem(2, FINE), vmem(2, FINE)]
    scratch += [vmem(2, FINE + 2), vmem(2, FINE + 2)]
    scratch += [vmem(2, MID + 2), vmem(6, 2, MID), vmem(2, MID), vmem(2, MID), vmem(2, MID)]
    scratch += [vmem(2, MID + 2), vmem(2, MID + 2)]
    scratch += [vmem(2, LOW + 2), vmem(6, 2, LOW), vmem(2, LOW), vmem(2, LOW)]
    scratch += [vmem(2, LOW + 2), vmem(2, LOW + 2)]
    scratch += [vmem(OWN2), pltpu.VMEM((8, LANES), jnp.float32), vmem(LOW + 1), vmem(SHIFTED)]
    scratch += [vmem(2), vmem(OWN2), vmem(2, 2), vmem(2, 8, 2), vmem(2), vmem(2, size_y - 1)]
    scratch += [vmem(2, 2), vmem(2, size_x - 1, 2)]
    scratch += [pltpu.SemaphoreType.DMA((18,))]
    whole = pl.BlockSpec(memory_space=pltpu.VMEM)
    done = pl.pallas_call(
        kernel,
        out_shape=jax.ShapeDtypeStruct(flat, jnp.float32),
        in_specs=[pl.BlockSpec(memory_space=pltpu.SMEM), whole, whole],
        out_specs=whole,
        scratch_shapes=scratch,
        compiler_params=pltpu.CompilerParams(
            collective_id=0, has_side_effects=True, vmem_limit_bytes=32 << 20
        ),
        name="cycles",
    )(strip_rows, source.reshape(flat), coefficient.reshape(flat))
    return done.reshape(source.shape)


def solution(mesh):
    placed = (P(None, "px", "py"), P(None, "px", "py"), P())
    return jax.shard_map(
        shards, mesh=mesh, in_specs=placed, out_specs=P(None, "px", "py"), check_vma=False
    )
```

time: 1150 us -> 59.7 us (0.05); the launches traced: 1130 us -> 59.6 us
  waiting for transfers between devices: 323 us -> 0 us
  starting transfers between devices: 256 us -> 0 us
  local copies, waits for them, and re-layouts: 240 us -> 3.12 us
  blocking collectives: 133 us -> 0 us
  other arithmetic: 114 us -> 0 us
  loops' own time: 57.7 us -> 0 us
  Pallas kernels: 0 us -> 56.5 us
    ppermute x84 -> x0, starting transfers between devices: 215 us -> none  [the longest x42 146 us: extended(): before = lax.ppermute(last, axis, up)]
    ppermute x84 -> x0, waiting for transfers between devices: 180 us -> none  [the longest x42 137 us: extended(): after = lax.ppermute(initial, axis, down)]
    all_to_all x4 -> x0, waiting for transfers between devices: 143 us -> none  [the longest x2 97.3 us: from_strips(): lax.all_to_all(strip_values[None], 'py', split_axis=3, concat_axis=0, til...]
    dynamic_update_slice x32 -> x0, local copies, waits for them, and re-layouts: 107 us -> none  [place_strip(): lax.dynamic_update_slice_in_dim(canvas_now, current + piece, first_row, 1)]
    all_to_all x1 -> x0, blocking collectives: 67 us -> none  [to_strips(): lax.all_to_all(pieces, 'py', split_axis=0, concat_axis=3, tiled=True)[0]]
    all_gather x3 -> x0, blocking collectives: 66.4 us -> none  [to_strips(): gathered = lax.all_gather(level_values, 'px', axis=1, tiled=True)]
    add x65 -> x0, other arithmetic: 60.9 us -> none  [the longest x23 38.4 us: relax_sweep(): values + relaxation * faces[7] * update(values, values_pad, faces, source...]
    another operation x2 -> x0, loops' own time: 57.7 us -> none  [from_strips(): canvas = lax.fori_loop(0, pieces_count, place_strip, canvas)]
  transfers between devices with their start and end apart: 88 -> 0, of which waited for: 48 -> 0; matrix products, arithmetic and copies ran while one was open for 4% -> 0% of each run, Pallas kernels for 0% -> 0%
where the time goes in v1:
time: 59.7 us; the launch traced here: 59.6 us
  Pallas kernels  56.5 us (95%)
  local copies, waits for them, and re-layouts  3.12 us (5%)
    pallas_call x1, Pallas kernels, shards(): pl.pallas_call(kernel, out_shape=jax.ShapeDtypeStruct(flat, jnp.float32),...  56.5 us
    unnamed x7, local copies, waits for them, and re-layouts  3.12 us

profile of v1, /device:TPU:1, one launch (start us, length us, event | category | flops | bytes accessed | tf_op | source)
XLA Modules:
  0.0 59.6 jit_solution(1421453557549318408)
XLA Ops:
  0.0 0.0 copy-start.2
  0.0 0.7 %copy-done.2 = s32[16]{0:T(128)S(1)} copy-done((s32[16]{0:T(128)S(1)}, s32[16]{0:T(128)}, u32[]{:S(2)}) %copy-start.2) | copy-done | bytes 88
  0.7 0.0 copy-start
  0.7 0.9 %copy-done = f32[8,32,128]{2,1,0:T(8,128)S(1)} copy-done((f32[8,32,128]{2,1,0:T(8,128)S(1)}, f32[8,32,128]{2,1,0:T(8,128)}, u32[]{:S(2)}) %copy-start) | copy-done | bytes 131096
  1.6 0.0 copy-start.1
  1.6 0.9 %copy-done.1 = f32[8,32,128]{2,1,0:T(8,128)S(1)} copy-done((f32[8,32,128]{2,1,0:T(8,128)S(1)}, f32[8,32,128]{2,1,0:T(8,128)}, u32[]{:S(2)}) %copy-start.1) | copy-done | bytes 131096
  2.5 56.5 %cycles.1 = f32[256,128]{1,0:T(8,128)S(1)} custom-call(s32[16]{0:T(128)S(1)} %copy-done.2, f32[256,128]{1,0:T(8,128)S(1)} %bitcast.4, f32[256,128]{1,0:T(8,128)S(1)} %bitcast.5), custom_call_target="tpu_custom_call" | custom-call | tf_op jit(solution)/shard_map/cycles/pallas_call | solution.py:604
  58.9 0.7 %copy.5 = f32[8,32,128]{2,1,0:T(8,128)} copy(f32[8,32,128]{2,1,0:T(8,128)S(1)} %bitcast.3) | data formatting | bytes 262144
Async XLA Ops:
  0.0 0.7 %copy-start.2 = (s32[16]{0:T(128)S(1)}, s32[16]{0:T(128)}, u32[]{:S(2)}) copy-start(s32[16]{0:T(128)} %strip_ref.1) | copy-start | bytes 196
  0.7 0.9 %copy-start = (f32[8,32,128]{2,1,0:T(8,128)S(1)}, f32[8,32,128]{2,1,0:T(8,128)}, u32[]{:S(2)}) copy-start(f32[8,32,128]{2,1,0:T(8,128)} %param.3) | copy-start | bytes 393220
  1.6 0.9 %copy-start.1 = (f32[8,32,128]{2,1,0:T(8,128)S(1)}, f32[8,32,128]{2,1,0:T(8,128)}, u32[]{:S(2)}) copy-start(f32[8,32,128]{2,1,0:T(8,128)} %param.4) | copy-start | bytes 393220

commit v2 on v1

v2 whole, which is shorter than its diff:
```python
import jax
import jax.numpy as jnp
from jax import lax
from jax.experimental import pallas as pl
from jax.experimental.pallas import tpu as pltpu
from jax.sharding import PartitionSpec as P

CYCLES = 2
COARSE_SWEEPS = 6
relaxation = 0.8
z_coupling = 0.25

MESH = pl.DeviceIdType.MESH

NZ = 8
ROWS = 32
LANES = 128
EDGE = 16
HALO = 12
FINE = ROWS + 2 * HALO
MID = FINE // 2
OWN2 = ROWS // 4
LOW_TILES = 3 * OWN2 // 2
MID_LANE, MID_OWN = 32, 64
LOW_LANE, LOW_OWN, HALF = 8, 32, 64


def lanes_of(rows):
    return lax.broadcasted_iota(jnp.int32, (rows, NZ, LANES), 2)


def layers_of(rows):
    return lax.broadcasted_iota(jnp.int32, (rows, NZ, LANES), 1)


def beside_lanes(parts, tiles):
    back = [pltpu.roll(part, 1, 2) for part in parts]
    ahead = [pltpu.roll(part, LANES - 1, 2) for part in parts]
    if len(parts) == 1:
        return back, ahead
    lane = lanes_of(parts[0].shape[0])
    before, after = lane < 1, lane >= LANES - 1
    south = [jnp.where(before, back[1 - t], back[t]) for t in tiles]
    north = [jnp.where(after, ahead[1 - t], ahead[t]) for t in tiles]
    return south, north


def six_sum(weights, t, here, west, own, east, south, north):
    total = weights[0, t, here] * west + weights[1, t, here] * east
    total += weights[4, t, here] * pltpu.roll(own, 1, 1)
    total += weights[5, t, here] * pltpu.roll(own, NZ - 1, 1)
    total += weights[2, t, here] * south
    total += weights[3, t, here] * north
    return total


def weighted(values, weights, row, rows, tiles):
    parts = [values[t, row + 1:row + 1 + rows] for t in range(values.shape[0])]
    south, north = beside_lanes(parts, tiles)
    totals = []
    for at, t in enumerate(tiles):
        west, east = values[t, row:row + rows], values[t, row + 2:row + 2 + rows]
        totals.append(six_sum(weights, t, slice(row, row + rows), west, parts[t], east,
                              south[at], north[at]))
    return [parts[t] for t in tiles], totals


def sweep(values, new, weights, right, first, count, rows):
    tiles = range(values.shape[0])
    for index in range(count):
        row = first + index * rows
        old, total = weighted(values, weights, row, rows, tiles)
        for t in tiles:
            new[t, row + 1:row + 1 + rows] = (
                right[t, row:row + rows] + (1.0 - relaxation) * old[t] + total[t])


def scaled_faces(own, west, east, south, north, z_factor, keep=None):
    layer = layers_of(own.shape[0])
    half_z = 0.5 * z_factor
    faces = [
        0.5 * (own + west), 0.5 * (own + east), 0.5 * (own + south), 0.5 * (own + north),
        jnp.where(layer > 0, half_z * (own + pltpu.roll(own, 1, 1)), 0.0),
        jnp.where(layer < NZ - 1, half_z * (own + pltpu.roll(own, NZ - 1, 1)), 0.0),
    ]
    diagonal = faces[0] + faces[1] + faces[2] + faces[3] + faces[4] + faces[5]
    inside = own > 0.0
    inverse = jnp.where(inside, relaxation / jnp.where(inside, diagonal, 1.0), 0.0)
    if keep is not None:
        faces[0], faces[1] = faces[0] * keep[0], faces[1] * keep[1]
    return [inverse * face for face in faces], inverse, diagonal


def make_weights(conduct, weights, row, rows, z_factor):
    tiles = range(conduct.shape[0])
    parts = [conduct[t, row + 1:row + 1 + rows] for t in tiles]
    south, north = beside_lanes(parts, tiles)
    inverses, diagonals = [], []
    for t in tiles:
        west, east = conduct[t, row:row + rows], conduct[t, row + 2:row + 2 + rows]
        faces, inverse, diagonal = scaled_faces(
            parts[t], west, east, south[t], north[t], z_factor)
        for side in range(6):
            weights[side, t, row:row + rows] = faces[side]
        inverses.append(inverse)
        diagonals.append(diagonal)
    return inverses, diagonals


def low_rows_beside(values):
    first = pltpu.roll(values[LOW_TILES - 1:], HALF, 2)
    last = pltpu.roll(values[:1], HALF, 2)
    west = jnp.concatenate([first, values[:-1]], axis=0)
    east = jnp.concatenate([values[1:], last], axis=0)
    return west, east


def low_sum(values, weights):
    west, east = low_rows_beside(values)
    back, ahead = pltpu.roll(values, 1, 2), pltpu.roll(values, LANES - 1, 2)
    return six_sum(weights, 0, slice(0, LOW_TILES), west, values, east, back, ahead)


def pair_rows(values):
    rows = values.shape[0]
    return jnp.sum(values.reshape(rows // 2, 2, NZ, LANES), axis=1)


def twice_rows(values):
    rows = values.shape[0]
    wide = jnp.broadcast_to(values[:, None], (rows, 2, NZ, LANES))
    return wide.reshape(2 * rows, NZ, LANES)


def select_lanes(values, chosen):
    rows = values.shape[0]
    flat = jnp.dot(
        values.reshape(rows * NZ, LANES), chosen, precision=lax.Precision.HIGHEST,
        preferred_element_type=jnp.float32)
    return flat.reshape(rows, NZ, LANES)


def roll_lanes(tile, amount):
    amount = amount % LANES
    return tile if amount == 0 else pltpu.roll(tile, amount, 1)


def pack_edges(block, group, right_side):
    lane = lax.broadcasted_iota(jnp.int32, (NZ, LANES), 1)
    packed = None
    for j in range(8):
        moved = roll_lanes(block[8 * group + j], EDGE * j + (EDGE if right_side else 0))
        packed = moved if packed is None else jnp.where(lane // EDGE == j, moved, packed)
    return packed


def unpack_edges(left, right, j):
    lane = lax.broadcasted_iota(jnp.int32, (NZ, LANES), 1)
    from_right = roll_lanes(right, -EDGE * j)
    from_left = roll_lanes(left, -EDGE * (j + 1))
    return jnp.where(lane < EDGE, from_right, jnp.where(lane >= LANES - EDGE, from_left, 0.0))


def pack_low(rows):
    out = rows[0]
    for m in range(1, 4):
        out = out + roll_lanes(rows[m], LOW_OWN * m)
    return out


def unpack_low(get, scale_left, scale_right, scale_rows):
    lane = lax.broadcasted_iota(jnp.int32, (NZ, LANES), 1)
    rows = []
    for a in (-1, 0, 1):
        for q in (0, 1):
            own = get(a, 0, q)
            left, right = roll_lanes(get(a, -1, q), -LOW_OWN), roll_lanes(get(a, 1, q), LOW_OWN)
            if scale_left is not None:
                left, right = left * scale_left, right * scale_right
            if scale_rows is not None and a != 0:
                scale = scale_rows[0 if a < 0 else 1]
                own, left, right = own * scale, left * scale, right * scale
            for m in range(4):
                row = len(rows)
                away = (lane - LOW_OWN * m) % LANES
                tile = jnp.where(
                    away < LOW_OWN, own,
                    jnp.where(away < LOW_OWN + LOW_LANE, right,
                              jnp.where(away >= LANES - LOW_LANE, left, 0.0)))
                half = HALF if row >= LOW_TILES else 0
                rows.append(roll_lanes(tile, half + LOW_LANE - LOW_OWN * m))
    return jnp.stack([rows[i] + rows[i + LOW_TILES] for i in range(LOW_TILES)])


class Exchange:
    def __init__(self, depth):
        self.depth = depth
        sizes = [depth] * 2 + [4] * 2 + [2] * 4
        self.at = [sum(sizes[:i]) for i in range(9)]

    def stage(self, edges, block):
        for side in (0, 1):
            for group in range(4):
                edges[side, group] = pack_edges(block, group, side == 1)

    def start(self, block, edges, got, send_sem, got_sem, near):
        n, at = self.depth, self.at
        top, bottom = pl.ds(0, 2), pl.ds(2, 2)
        moves = [
            (block.at[pl.ds(ROWS - n, n)], 0, (1, 0)),
            (block.at[pl.ds(0, n)], 1, (-1, 0)),
            (edges.at[1], 2, (0, 1)),
            (edges.at[0], 3, (0, -1)),
            (edges.at[1, bottom], 4, (1, 1)),
            (edges.at[0, bottom], 5, (1, -1)),
            (edges.at[1, top], 6, (-1, 1)),
            (edges.at[0, top], 7, (-1, -1)),
        ]
        for source, slot, way in moves:
            pltpu.make_async_remote_copy(
                src_ref=source,
                dst_ref=got.at[pl.ds(at[slot], at[slot + 1] - at[slot])],
                send_sem=send_sem,
                recv_sem=got_sem,
                device_id=near(*way),
                device_id_type=MESH,
            ).start()

    def unpack(self, got, put_rows, put_beside):
        n, at = self.depth, self.at
        put_rows(HALO - n, n, got[at[0]:at[0] + n])
        put_rows(HALO + ROWS, n, got[at[1]:at[1] + n])
        for i in range(FINE):
            if i < HALO:
                source = ROWS - HALO + i
                offset = at[4] - 2, at[5] - 2
            elif i < HALO + ROWS:
                source = i - HALO
                offset = at[2], at[3]
            else:
                source = i - HALO - ROWS
                offset = at[6], at[7]
            group, j = divmod(source, 8)
            put_beside(i, unpack_edges(got[offset[0] + group], got[offset[1] + group], j))


AROUND = [(a, b) for a in (-1, 0, 1) for b in (-1, 0, 1) if (a, b) != (0, 0)]
FOR_K, FOR_F, FOR_S = Exchange(HALO), Exchange(HALO - 2), Exchange(HALO - 1)


def kernel(strip_ref, source_ref, coefficient_ref, out_ref,
           k_in, f_in, k_own, f_own, s_own, k_edge, f_edge, s_edge, k_got, f_got, s_got,
           k0, c0, g0, d0, va, vb, k1, c1, i1, g1, d1, ua, ub, k2, c2, i2,
           weight, shifts, pick, l_own, l_send, l_got, one_send, one_got, two_send, two_got,
           picked, sems):
    px, py = lax.axis_index("px"), lax.axis_index("py")
    size_x, size_y = lax.axis_size("px"), lax.axis_size("py")
    strips = strip_ref.shape[0]

    def near(a, b):
        return (lax.rem(px + a + size_x, size_x), lax.rem(py + b + size_y, size_y))

    k_copy = pltpu.make_async_copy(coefficient_ref, k_in, sems.at[0])
    f_copy = pltpu.make_async_copy(source_ref, f_in, sems.at[1])
    k_copy.start()
    f_copy.start()
    peers = [(0, b) for b in range(1, size_y)] + [(a, 0) for a in range(1, size_x)]
    peers += [way for way in AROUND if way[0] and way[1]]
    barrier = pltpu.get_barrier_semaphore()
    for way in peers:
        pl.semaphore_signal(barrier, inc=1, device_id=near(*way), device_id_type=MESH)

    def arrived(buffer, sem):
        pltpu.make_async_copy(buffer, buffer, sem).wait()

    def spread(source, got, sem, ways):
        for slot, way in enumerate(ways):
            pltpu.make_async_remote_copy(
                src_ref=source,
                dst_ref=got.at[slot],
                send_sem=sems.at[sem],
                recv_sem=sems.at[sem + 1],
                device_id=near(*way),
                device_id_type=MESH,
            ).start()

    one = lax.broadcasted_iota(jnp.int32, (LANES, LANES), 0)
    other = lax.broadcasted_iota(jnp.int32, (LANES, LANES), 1)

    def chosen(condition):
        return jnp.where(condition, 1.0, 0.0)

    def beside_pairs(wide, narrow):
        nearby = (wide < EDGE) & (narrow == MID_LANE + MID_OWN + wide // 2)
        return nearby | ((wide >= LANES - EDGE) & (narrow == MID_LANE - LANES // 2 + wide // 2))

    def low_of(mid, half):
        return half + LOW_LANE - MID_LANE // 2 + mid // 2

    mid_halo = 2 * LOW_LANE
    mid_in = (other >= MID_LANE - mid_halo) & (other < MID_LANE + MID_OWN + mid_halo)
    tables = [
        chosen(other == MID_LANE + one // 2), chosen(beside_pairs(one, other)),
        chosen(one == MID_LANE + other // 2), chosen(beside_pairs(other, one)),
        chosen((one >= MID_LANE) & (one < MID_LANE + MID_OWN)
               & (other == (one - MID_LANE) // 2)),
        chosen(mid_in & (one == low_of(other, 0))), chosen(mid_in & (one == low_of(other, HALF))),
        chosen(other == one // 4),
    ]
    for at, table in enumerate(tables):
        picked[at] = table

    ends, total = [], jnp.int32(0)
    for c in range(strips):
        total = total + strip_ref[c]
        ends.append(total)
    sub = lax.broadcasted_iota(jnp.int32, (8, LANES), 0)
    lane = lax.broadcasted_iota(jnp.int32, (8, LANES), 1)

    def strip_of(rows):
        found = jnp.zeros_like(rows)
        for end in ends:
            found = found + jnp.where(rows >= end, 1, 0)
        return found

    lane_strip = strip_of(lane)
    for tile in (0, 1):
        rows = jnp.clip(OWN2 * px - 4 + 8 * tile + sub, 0, OWN2 * size_x - 1)
        pick[tile] = jnp.where(strip_of(rows) == lane_strip, 1.0, 0.0)

    zero = jnp.zeros((NZ, LANES), jnp.float32)
    for ref, end in ((k0, FINE), (va, FINE), (vb, FINE), (k1, MID), (ua, MID), (ub, MID)):
        for t in range(ref.shape[0]):
            ref[t, 0] = zero
            ref[t, end + 1] = zero
    for i in (0, 1, FINE - 2, FINE - 1):
        va[0, 1 + i] = zero

    k_copy.wait()
    for r in range(ROWS):
        k_own[r] = k_in[pl.ds(r, NZ, stride=ROWS), :]
    lows = (1.0 / 16.0) * select_lanes(pair_rows(pair_rows(k_own[...])), picked[7])
    for q in (0, 1):
        l_send[2, q] = pack_low([lows[4 * q + m] for m in range(4)])
    FOR_K.stage(k_edge, k_own)
    f_copy.wait()
    for r in range(ROWS):
        f_own[r] = f_in[pl.ds(r, NZ, stride=ROWS), :]
    FOR_F.stage(f_edge, f_own)
    pl.semaphore_wait(barrier, len(peers))
    outward = [(-a, -b) for a, b in AROUND]
    spread(l_send.at[2], l_got.at[2], 2, outward)
    FOR_K.start(k_own, k_edge, k_got, sems.at[4], sems.at[5], near)
    FOR_F.start(f_own, f_edge, f_got, sems.at[6], sems.at[7], near)

    wide_lane = lax.broadcasted_iota(jnp.int32, (NZ, LANES), 1)
    in_left, in_right = jnp.where(py > 0, 1.0, 0.0), jnp.where(py < size_y - 1, 1.0, 0.0)
    inner_y = jnp.where(wide_lane < LANES // 2, in_right, in_left)
    row_in = [jnp.where(px > 0, 1.0, 0.0), jnp.where(px < size_x - 1, 1.0, 0.0)]

    kept = []
    for tile in range(4):
        rows = OWN2 * px - OWN2 + 8 * tile + sub
        flags = jnp.ones((8, LANES), jnp.float32)
        for end in ends:
            flags = jnp.where(rows == end, 0.0, flags)
        kept += [jnp.broadcast_to(flags[i:i + 1], (NZ, LANES)) for i in range(8)]
    lower_half = wide_lane < HALF
    keep = [
        jnp.stack([jnp.where(lower_half, kept[i + d], kept[i + d + LOW_TILES])
                   for i in range(LOW_TILES)]) for d in (0, 1)]

    def tiles_of(at):
        return lambda a, b, q: (
            l_send[at, q] if (a, b) == (0, 0) else l_got[at, AROUND.index((a, b)), q])

    arrived(l_got.at[2], sems.at[3])
    lows = unpack_low(tiles_of(2), in_left, in_right, row_in)
    k2[...] = lows
    west, east = low_rows_beside(lows)
    faces, inverse, diagonal = scaled_faces(
        lows, west, east, pltpu.roll(lows, 1, 2), pltpu.roll(lows, LANES - 1, 2),
        16.0 * z_coupling, keep)
    for side in range(6):
        c2[side, 0] = faces[side]
    i2[...] = inverse
    ones = jnp.where(lows > 0.0, 1.0, 0.0)
    for turn in range(COARSE_SWEEPS):
        ones = (1.0 - relaxation) * ones + low_sum(ones, c2)

    def own_low(values):
        out = []
        for r in range(OWN2, 2 * OWN2):
            half = HALF if r >= LOW_TILES else 0
            moved = roll_lanes(values[r % LOW_TILES], -half - LOW_LANE)
            out.append(jnp.where(wide_lane < LOW_OWN, moved, 0.0))
        return jnp.stack(out)

    weight[...] = own_low(ones)

    def in_row(values):
        column = jnp.sum(jnp.sum(values, axis=1), axis=1, keepdims=True)
        return jnp.sum(jnp.where(lane == OWN2 * px + sub, column, 0.0), axis=0, keepdims=True)

    one_send[0, 1] = in_row(own_low(diagonal))

    def put_k_rows(first, rows, values):
        k0[0, 1 + first:1 + first + rows] = values * row_in[0 if first < HALO else 1]

    def put_k_beside(i, tile):
        tile = tile * inner_y
        if i < HALO or i >= HALO + ROWS:
            tile = tile * row_in[0 if i < HALO else 1]
        k0[1, 1 + i] = tile

    k0[0, 1 + HALO:1 + HALO + ROWS] = k_own[...]
    arrived(k_got, sems.at[5])
    FOR_K.unpack(k_got, put_k_rows, put_k_beside)

    def restrict(parts):
        total = select_lanes(pair_rows(parts[0]), picked[0])
        return total + select_lanes(pair_rows(parts[1]), picked[1])

    for row in range(0, FINE, 8):
        inverse, diagonal = make_weights(k0, c0, row, 8, z_coupling)
        for t in (0, 1):
            g0[t, row:row + 8] = inverse[t]
            d0[t, row:row + 8] = (1.0 / relaxation) * diagonal[t]
        k1[0, row // 2 + 1:row // 2 + 5] = 0.25 * restrict(
            [k0[t, row + 1:row + 9] for t in (0, 1)])
    for row in range(0, MID, 7):
        inverse, diagonal = make_weights(k1, c1, row, 7, 4.0 * z_coupling)
        i1[0, row:row + 7] = inverse[0]
        d1[0, row:row + 7] = (1.0 / relaxation) * diagonal[0]

    va[0, 1 + HALO:1 + HALO + ROWS] = f_own[...]

    def put_f_rows(first, rows, values):
        va[0, 1 + first:1 + first + rows] = values

    def put_f_beside(i, tile):
        va[1, 1 + i] = tile

    arrived(f_got, sems.at[7])
    FOR_F.unpack(f_got, put_f_rows, put_f_beside)
    for row in range(0, FINE, 8):
        for t in (0, 1):
            start = g0[t, row:row + 8] * va[t, row + 1:row + 9]
            g0[t, row:row + 8] = start
            va[t, row + 1:row + 9] = start

    dens = None
    used = 8
    for cycle in range(CYCLES):
        if cycle > 0:
            sweep(va, vb, c0, g0, 0, FINE // 8, 8)
            sweep(vb, va, c0, g0, 0, FINE // 8, 8)
            fine, spare = va, vb
        else:
            sweep(va, vb, c0, g0, 0, FINE // 8, 8)
            fine, spare = vb, va

        for row in range(0, FINE, 8):
            old, total = weighted(fine, c0, row, 8, (0, 1))
            rest = [
                d0[t, row:row + 8] * (g0[t, row:row + 8] - relaxation * old[t] + total[t])
                for t in (0, 1)]
            half = row // 2
            start = i1[0, half:half + 4] * restrict(rest)
            g1[0, half:half + 4] = start
            ua[0, half + 1:half + 5] = start
        sweep(ua, ub, c1, g1, 0, MID // 7, 7)
        for part in (0, 1):
            row = HALO // 2 + 8 * part
            old, total = weighted(ub, c1, row, 8, (0,))
            rest = d1[0, row:row + 8] * (
                g1[0, row:row + 8] - relaxation * old[0] + total[0])
            l_own[4 * part:4 * part + 4] = select_lanes(pair_rows(rest), picked[4])

        one_send[cycle, 0] = in_row(weight[...] * l_own[...])
        wide = 2 if cycle == 0 else 1
        one_out, one_in = one_send.at[cycle, pl.ds(0, wide)], one_got.at[cycle, :, pl.ds(0, wide)]
        two_out, two_in = two_send.at[cycle, pl.ds(0, wide)], two_got.at[cycle, :, pl.ds(0, wide)]
        spread(one_out, one_in, used, [(0, b) for b in range(1, size_y)])
        for q in (0, 1):
            l_send[cycle, q] = pack_low([l_own[4 * q + m] for m in range(4)])
        spread(l_send.at[cycle], l_got.at[cycle], used + 2, outward)
        arrived(one_in, sems.at[used + 1])
        for part in range(wide):
            two_send[cycle, part] = one_send[cycle, part] + jnp.sum(one_got[cycle, :, part], axis=0)
        spread(two_out, two_in, used + 4, [(a, 0) for a in range(1, size_x)])

        arrived(l_got.at[cycle], sems.at[used + 3])
        right = i2[...] * unpack_low(tiles_of(cycle), None, None, None)
        low = right
        for turn in range(COARSE_SWEEPS - 1):
            low = right + (1.0 - relaxation) * low + low_sum(low, c2)

        arrived(two_in, sems.at[used + 5])
        parts = []
        for part in range(wide):
            both = two_send[cycle, part] + jnp.sum(two_got[cycle, :, part], axis=0)
            row_sums = jnp.broadcast_to(both, (8, LANES))
            parts.append([jnp.sum(pick[tile] * row_sums, axis=1, keepdims=True) for tile in (0, 1)])
        if cycle == 0:
            dens = parts[1]
        for tile in (0, 1):
            shift = jnp.broadcast_to(parts[0][tile] / dens[tile], (8, LANES))
            for i in range(8):
                shifts[8 * tile + i] = jnp.broadcast_to(shift[i:i + 1], (NZ, LANES))

        for part in (0, 1):
            tiles = slice(6, LOW_TILES) if part == 0 else slice(0, 6)
            moved = jnp.where(k2[tiles] > 0.0, shifts[2 + 6 * part:8 + 6 * part], 0.0)
            wave = select_lanes(low[tiles] + moved, picked[5 + part])
            at = 3 + 12 * part
            ua[0, at:at + 12] = ub[0, at:at + 12] + twice_rows(wave)
        sweep(ua, ub, c1, g1, 2, 3, 8)
        sweep(ub, ua, c1, g1, 2, 3, 8)

        for row in range(8, 48, 8):
            wave = ua[0, row // 2 + 1:row // 2 + 5]
            for t in (0, 1):
                spare[t, row + 1:row + 9] = fine[t, row + 1:row + 9] + twice_rows(
                    select_lanes(wave, picked[2 + t]))
        sweep(spare, fine, c0, g0, 8, 5, 8)
        for part in range(ROWS // 8):
            row = HALO + 8 * part
            old, total = weighted(fine, c0, row, 8, (0,))
            s_own[8 * part:8 * part + 8] = (
                g0[0, row:row + 8] + (1.0 - relaxation) * old[0] + total[0])
        used += 6

        if cycle < CYCLES - 1:
            FOR_S.stage(s_edge, s_own)
            FOR_S.start(s_own, s_edge, s_got, sems.at[used], sems.at[used + 1], near)
            va[0, 1 + HALO:1 + HALO + ROWS] = s_own[...]
            va[0, 1] = zero
            va[0, FINE] = zero

            def put_s_rows(first, rows, values):
                inside = k0[0, 1 + first:1 + first + rows] > 0.0
                va[0, 1 + first:1 + first + rows] = jnp.where(inside, values, 0.0)

            def put_s_beside(i, tile):
                va[1, 1 + i] = jnp.where(k0[1, 1 + i] > 0.0, tile, 0.0)

            arrived(s_got, sems.at[used + 1])
            FOR_S.unpack(s_got, put_s_rows, put_s_beside)
            arrived(s_got, sems.at[used])
            used += 2

    for r in range(ROWS):
        out_ref[pl.ds(r, NZ, stride=ROWS), :] = s_own[r]

    arrived(l_got.at[2], sems.at[2])
    arrived(k_got, sems.at[4])
    arrived(f_got, sems.at[6])
    for cycle, at in ((0, 8), (1, 16)):
        wide = pl.ds(0, 2 - cycle)
        arrived(one_got.at[cycle, :, wide], sems.at[at])
        arrived(l_got.at[cycle], sems.at[at + 2])
        arrived(two_got.at[cycle, :, wide], sems.at[at + 4])


def vmem(*shape):
    return pltpu.VMEM(shape + (NZ, LANES), jnp.float32)


def shards(source, coefficient, strip_rows):
    size_x, size_y = lax.axis_size("px"), lax.axis_size("py")
    flat = (NZ * ROWS, LANES)
    scratch = [pltpu.VMEM(flat, jnp.float32)] * 2
    scratch += [vmem(ROWS), vmem(ROWS), vmem(ROWS), vmem(2, 4), vmem(2, 4), vmem(2, 4)]
    scratch += [vmem(e.at[8]) for e in (FOR_K, FOR_F, FOR_S)]
    scratch += [vmem(2, FINE + 2), vmem(6, 2, FINE), vmem(2, FINE), vmem(2, FINE)]
    scratch += [vmem(2, FINE + 2), vmem(2, FINE + 2)]
    scratch += [vmem(1, MID + 2), vmem(6, 1, MID), vmem(1, MID), vmem(1, MID), vmem(1, MID)]
    scratch += [vmem(1, MID + 2), vmem(1, MID + 2)]
    scratch += [vmem(LOW_TILES), vmem(6, 1, LOW_TILES), vmem(LOW_TILES)]
    scratch += [vmem(OWN2), vmem(16), vmem(2), vmem(OWN2), vmem(3, 2), vmem(3, 8, 2)]
    row = lambda *shape: pltpu.VMEM(shape + (1, LANES), jnp.float32)
    scratch += [row(2, 2), row(2, size_y - 1, 2), row(2, 2), row(2, size_x - 1, 2)]
    scratch += [pltpu.VMEM((8, LANES, LANES), jnp.float32), pltpu.SemaphoreType.DMA((22,))]
    hbm = pl.BlockSpec(memory_space=pltpu.HBM)
    done = pl.pallas_call(
        kernel,
        out_shape=jax.ShapeDtypeStruct(flat, jnp.float32),
        in_specs=[pl.BlockSpec(memory_space=pltpu.SMEM), hbm, hbm],
        out_specs=pl.BlockSpec(memory_space=pltpu.VMEM),
        scratch_shapes=scratch,
        compiler_params=pltpu.CompilerParams(
            collective_id=0, has_side_effects=True, vmem_limit_bytes=32 << 20
        ),
        name="cycles",
    )(strip_rows, source.reshape(flat), coefficient.reshape(flat))
    return done.reshape(source.shape)


def solution(mesh):
    placed = (P(None, "px", "py"), P(None, "px", "py"), P())
    return jax.shard_map(
        shards, mesh=mesh, in_specs=placed, out_specs=P(None, "px", "py"), check_vma=False
    )
```

time: 59.7 us -> 49.7 us (0.83)
  Pallas kernels: 56.5 us -> 46.5 us
    pallas_call x1, Pallas kernels: 56.5 us -> 46.5 us  [shards(): pl.pallas_call(kernel, out_shape=jax.ShapeDtypeStruct(flat, jnp.float32),...]
where the time goes in v2:
time: 49.7 us; the launch traced here: 49.6 us
  Pallas kernels  46.5 us (94%)
  local copies, waits for them, and re-layouts  3.12 us (6%)
    pallas_call x1, Pallas kernels, shards(): pl.pallas_call(kernel, out_shape=jax.ShapeDtypeStruct(flat, jnp.float32),...  46.5 us
    unnamed x7, local copies, waits for them, and re-layouts  3.12 us

profile of v2, /device:TPU:1, one launch (start us, length us, event | category | flops | bytes accessed | tf_op | source)
XLA Modules:
  0.0 49.6 jit_solution(13084662432644352495)
XLA Ops:
  0.0 0.0 copy-start.2
  0.0 0.7 %copy-done.2 = s32[16]{0:T(128)S(1)} copy-done((s32[16]{0:T(128)S(1)}, s32[16]{0:T(128)}, u32[]{:S(2)}) %copy-start.2) | copy-done | bytes 88
  0.7 0.0 copy-start
  0.7 0.9 %copy-done = f32[8,32,128]{2,1,0:T(8,128)S(1)} copy-done((f32[8,32,128]{2,1,0:T(8,128)S(1)}, f32[8,32,128]{2,1,0:T(8,128)}, u32[]{:S(2)}) %copy-start) | copy-done | bytes 131096
  1.6 0.0 copy-start.1
  1.6 0.9 %copy-done.1 = f32[8,32,128]{2,1,0:T(8,128)S(1)} copy-done((f32[8,32,128]{2,1,0:T(8,128)S(1)}, f32[8,32,128]{2,1,0:T(8,128)}, u32[]{:S(2)}) %copy-start.1) | copy-done | bytes 131096
  2.5 46.5 %cycles.1 = f32[256,128]{1,0:T(8,128)S(1)} custom-call(s32[16]{0:T(128)S(1)} %copy-done.2, f32[256,128]{1,0:T(8,128)S(1)} %bitcast.4, f32[256,128]{1,0:T(8,128)S(1)} %bitcast.5), custom_call_target="tpu_custom_call" | custom-call | tf_op jit(solution)/shard_map/cycles/pallas_call | solution.py:586
  49.0 0.7 %copy.5 = f32[8,32,128]{2,1,0:T(8,128)} copy(f32[8,32,128]{2,1,0:T(8,128)S(1)} %bitcast.3) | data formatting | bytes 262144
Async XLA Ops:
  0.0 0.7 %copy-start.2 = (s32[16]{0:T(128)S(1)}, s32[16]{0:T(128)}, u32[]{:S(2)}) copy-start(s32[16]{0:T(128)} %strip_ref.1) | copy-start | bytes 196
  0.7 0.9 %copy-start = (f32[8,32,128]{2,1,0:T(8,128)S(1)}, f32[8,32,128]{2,1,0:T(8,128)}, u32[]{:S(2)}) copy-start(f32[8,32,128]{2,1,0:T(8,128)} %param.3) | copy-start | bytes 393220
  1.6 0.9 %copy-start.1 = (f32[8,32,128]{2,1,0:T(8,128)S(1)}, f32[8,32,128]{2,1,0:T(8,128)}, u32[]{:S(2)}) copy-start(f32[8,32,128]{2,1,0:T(8,128)} %param.4) | copy-start | bytes 393220

commit v3 on v2

--- a/solution.py
+++ b/solution.py
@@ -16,13 +16,14 @@
 ROWS = 32
 LANES = 128
 EDGE = 16
-HALO = 12
+HALO = 14
 FINE = ROWS + 2 * HALO
 MID = FINE // 2
 OWN2 = ROWS // 4
 LOW_TILES = 3 * OWN2 // 2
 MID_LANE, MID_OWN = 32, 64
 LOW_LANE, LOW_OWN, HALF = 8, 32, 64
+MID_HALO, MID_ROWS = HALO // 2, ROWS // 2
 
 
 def lanes_of(rows):
@@ -65,10 +66,13 @@
     return [parts[t] for t in tiles], totals
 
 
-def sweep(values, new, weights, right, first, count, rows):
+def groups(first, end, rows=8):
+    return [(row, min(rows, end - row)) for row in range(first, end, rows)]
+
+
+def sweep(values, new, weights, right, first, end):
     tiles = range(values.shape[0])
-    for index in range(count):
-        row = first + index * rows
+    for row, rows in groups(first, end):
         old, total = weighted(values, weights, row, rows, tiles)
         for t in tiles:
             new[t, row + 1:row + 1 + rows] = (
@@ -192,6 +196,47 @@
     return jnp.stack([rows[i] + rows[i + LOW_TILES] for i in range(LOW_TILES)])
 
 
+def pack_mid(rows):
+    lane = lax.broadcasted_iota(jnp.int32, (NZ, LANES), 1)
+    return [
+        jnp.where(lane < HALF, roll_lanes(rows[2 * j], -MID_LANE),
+                  roll_lanes(rows[2 * j + 1], MID_LANE)) for j in range(MID_ROWS // 2)]
+
+
+MID_AT, MID_TILES = {}, 0
+for side in [(a, b) for a in (-1, 0, 1) for b in (-1, 0, 1) if (a, b) != (0, 0)]:
+    MID_AT[side] = MID_TILES
+    MID_TILES += MID_ROWS // 2 if side[0] == 0 else MID_ROWS // 4
+
+
+def start_mid(send, got, send_sem, got_sem, near):
+    for a, b in AROUND:
+        count = MID_ROWS // 2 if a == 0 else MID_ROWS // 4
+        pltpu.make_async_remote_copy(
+            src_ref=send.at[pl.ds(MID_ROWS // 4 if a < 0 else 0, count)],
+            dst_ref=got.at[pl.ds(MID_AT[a, b], count)],
+            send_sem=send_sem,
+            recv_sem=got_sem,
+            device_id=near(-a, -b),
+            device_id_type=MESH,
+        ).start()
+
+
+def unpack_mid(got, which, put):
+    lane = lax.broadcasted_iota(jnp.int32, (NZ, LANES), 1)
+    own = (lane >= MID_LANE) & (lane < MID_LANE + MID_OWN)
+    for row in range(MID):
+        a = -1 if row < MID_HALO else 0 if row < MID_HALO + MID_ROWS else 1
+        source = row - MID_HALO - MID_ROWS * a
+        tile, half = divmod(source - (MID_ROWS // 2 if a < 0 else 0), 2)
+        turn = MID_LANE if half == 0 else -MID_LANE
+        left, right = got[MID_AT[a, -1] + tile, which], got[MID_AT[a, 1] + tile, which]
+        beside = roll_lanes(jnp.where(lane % HALF < MID_LANE, right, left), -turn)
+        if a != 0:
+            beside = jnp.where(own, roll_lanes(got[MID_AT[a, 0] + tile, which], turn), beside)
+        put(row, a, own, beside)
+
+
 class Exchange:
     def __init__(self, depth):
         self.depth = depth
@@ -244,14 +289,15 @@
             put_beside(i, unpack_edges(got[offset[0] + group], got[offset[1] + group], j))
 
 
-AROUND = [(a, b) for a in (-1, 0, 1) for b in (-1, 0, 1) if (a, b) != (0, 0)]
-FOR_K, FOR_F, FOR_S = Exchange(HALO), Exchange(HALO - 2), Exchange(HALO - 1)
-
-
-def kernel(strip_ref, source_ref, coefficient_ref, out_ref,
-           k_in, f_in, k_own, f_own, s_own, k_edge, f_edge, s_edge, k_got, f_got, s_got,
+AROUND = [(a, b) for a in (-1, 1) for b in (-1, 1)] + [(-1, 0), (1, 0), (0, -1), (0, 1)]
+FOR_K, FOR_F = Exchange(HALO), Exchange(HALO - 4)
+THIN = HALO - FOR_F.depth
+
+
+def kernel(strip_hbm, source_ref, coefficient_ref, out_ref,
+           strip_ref, k_in, f_in, k_own, f_own, s_own, k_edge, f_edge, k_got, f_got,
            k0, c0, g0, d0, va, vb, k1, c1, i1, g1, d1, ua, ub, k2, c2, i2,
-           weight, shifts, pick, l_own, l_send, l_got, one_send, one_got, two_send, two_got,
+           weight, shifts, pick, l_own, l_send, l_got, m_send, m_got, n_send, n_got, one_send, one_got, two_send, two_got,
            picked, sems):
     px, py = lax.axis_index("px"), lax.axis_index("py")
     size_x, size_y = lax.axis_size("px"), lax.axis_size("py")
@@ -262,10 +308,19 @@
 
     k_copy = pltpu.make_async_copy(coefficient_ref, k_in, sems.at[0])
     f_copy = pltpu.make_async_copy(source_ref, f_in, sems.at[1])
+    strip_copy = pltpu.make_async_copy(strip_hbm, strip_ref, sems.at[26])
     k_copy.start()
+    strip_copy.start()
     f_copy.start()
-    peers = [(0, b) for b in range(1, size_y)] + [(a, 0) for a in range(1, size_x)]
-    peers += [way for way in AROUND if way[0] and way[1]]
+    def around_ring(offset, size):
+        return min(offset % size, -offset % size)
+
+    along_y = sorted(range(1, size_y), key=lambda b: -around_ring(b, size_y))
+    along_x = sorted(
+        range(1, size_x),
+        key=lambda a: -around_ring(a % 4, 4) - around_ring((a + 1) // 4, size_x // 4))
+    to_y, to_x = [(0, b) for b in along_y], [(a, 0) for a in along_x]
+    peers = to_y + to_x + [way for way in AROUND if way[0] and way[1]]
     barrier = pltpu.get_barrier_semaphore()
     for way in peers:
         pl.semaphore_signal(barrier, inc=1, device_id=near(*way), device_id_type=MESH)
@@ -310,6 +365,7 @@
     for at, table in enumerate(tables):
         picked[at] = table
 
+    strip_copy.wait()
     ends, total = [], jnp.int32(0)
     for c in range(strips):
         total = total + strip_ref[c]
@@ -333,8 +389,11 @@
         for t in range(ref.shape[0]):
             ref[t, 0] = zero
             ref[t, end + 1] = zero
-    for i in (0, 1, FINE - 2, FINE - 1):
+    for i in range(THIN):
         va[0, 1 + i] = zero
+        va[0, FINE - i] = zero
+    for i in range(MID):
+        ua[0, 1 + i] = zero
 
     k_copy.wait()
     for r in range(ROWS):
@@ -421,17 +480,18 @@
         total = select_lanes(pair_rows(parts[0]), picked[0])
         return total + select_lanes(pair_rows(parts[1]), picked[1])
 
-    for row in range(0, FINE, 8):
-        inverse, diagonal = make_weights(k0, c0, row, 8, z_coupling)
+    for row, rows in groups(0, FINE, 10):
+        k1[0, row // 2 + 1:(row + rows) // 2 + 1] = 0.25 * restrict(
+            [k0[t, row + 1:row + rows + 1] for t in (0, 1)])
+    for row, rows in groups(THIN, FINE - THIN):
+        inverse, diagonal = make_weights(k0, c0, row, rows, z_coupling)
         for t in (0, 1):
-            g0[t, row:row + 8] = inverse[t]
-            d0[t, row:row + 8] = (1.0 / relaxation) * diagonal[t]
-        k1[0, row // 2 + 1:row // 2 + 5] = 0.25 * restrict(
-            [k0[t, row + 1:row + 9] for t in (0, 1)])
-    for row in range(0, MID, 7):
-        inverse, diagonal = make_weights(k1, c1, row, 7, 4.0 * z_coupling)
-        i1[0, row:row + 7] = inverse[0]
-        d1[0, row:row + 7] = (1.0 / relaxation) * diagonal[0]
+            g0[t, row:row + rows] = inverse[t]
+            d0[t, row:row + rows] = (1.0 / relaxation) * diagonal[t]
+    for row, rows in groups(0, MID, 10):
+        inverse, diagonal = make_weights(k1, c1, row, rows, 4.0 * z_coupling)
+        i1[0, row:row + rows] = inverse[0]
+        d1[0, row:row + rows] = (1.0 / relaxation) * diagonal[0]
 
     va[0, 1 + HALO:1 + HALO + ROWS] = f_own[...]
 
@@ -443,35 +503,41 @@
 
     arrived(f_got, sems.at[7])
     FOR_F.unpack(f_got, put_f_rows, put_f_beside)
-    for row in range(0, FINE, 8):
+    for row, rows in groups(THIN, FINE - THIN):
         for t in (0, 1):
-            start = g0[t, row:row + 8] * va[t, row + 1:row + 9]
-            g0[t, row:row + 8] = start
-            va[t, row + 1:row + 9] = start
+            start = g0[t, row:row + rows] * va[t, row + 1:row + rows + 1]
+            g0[t, row:row + rows] = start
+            va[t, row + 1:row + rows + 1] = start
+
+    def rows_0(halo):
+        return HALO - halo, HALO + ROWS + halo
+
+    def rows_1(halo):
+        return MID_HALO - halo, MID_HALO + MID_ROWS + halo
 
     dens = None
     used = 8
     for cycle in range(CYCLES):
         if cycle > 0:
-            sweep(va, vb, c0, g0, 0, FINE // 8, 8)
-            sweep(vb, va, c0, g0, 0, FINE // 8, 8)
+            sweep(va, vb, c0, g0, *rows_0(6))
+            sweep(vb, va, c0, g0, *rows_0(6))
             fine, spare = va, vb
         else:
-            sweep(va, vb, c0, g0, 0, FINE // 8, 8)
+            sweep(va, vb, c0, g0, *rows_0(10))
             fine, spare = vb, va
 
-        for row in range(0, FINE, 8):
-            old, total = weighted(fine, c0, row, 8, (0, 1))
+        for row, rows in groups(*rows_0(4)):
+            old, total = weighted(fine, c0, row, rows, (0, 1))
+            here = slice(row, row + rows)
             rest = [
-                d0[t, row:row + 8] * (g0[t, row:row + 8] - relaxation * old[t] + total[t])
-                for t in (0, 1)]
-            half = row // 2
-            start = i1[0, half:half + 4] * restrict(rest)
-            g1[0, half:half + 4] = start
-            ua[0, half + 1:half + 5] = start
-        sweep(ua, ub, c1, g1, 0, MID // 7, 7)
+                d0[t, here] * (g0[t, here] - relaxation * old[t] + total[t]) for t in (0, 1)]
+            half, count = row // 2, rows // 2
+            start = i1[0, half:half + count] * restrict(rest)
+            g1[0, half:half + count] = start
+            ua[0, half + 1:half + count + 1] = start
+        sweep(ua, ub, c1, g1, *rows_1(2))
         for part in (0, 1):
-            row = HALO // 2 + 8 * part
+            row = MID_HALO + 8 * part
             old, total = weighted(ub, c1, row, 8, (0,))
             rest = d1[0, row:row + 8] * (
                 g1[0, row:row + 8] - relaxation * old[0] + total[0])
@@ -481,20 +547,52 @@
         wide = 2 if cycle == 0 else 1
         one_out, one_in = one_send.at[cycle, pl.ds(0, wide)], one_got.at[cycle, :, pl.ds(0, wide)]
         two_out, two_in = two_send.at[cycle, pl.ds(0, wide)], two_got.at[cycle, :, pl.ds(0, wide)]
-        spread(one_out, one_in, used, [(0, b) for b in range(1, size_y)])
+        spread(one_out, one_in, used, to_y)
         for q in (0, 1):
             l_send[cycle, q] = pack_low([l_own[4 * q + m] for m in range(4)])
         spread(l_send.at[cycle], l_got.at[cycle], used + 2, outward)
-        arrived(one_in, sems.at[used + 1])
-        for part in range(wide):
-            two_send[cycle, part] = one_send[cycle, part] + jnp.sum(one_got[cycle, :, part], axis=0)
-        spread(two_out, two_in, used + 4, [(a, 0) for a in range(1, size_x)])
+        mids_out, mids_in = (m_send, m_got) if cycle == 0 else (n_send, n_got)
+        for j, tile in enumerate(pack_mid(ub[0, 1 + MID_HALO:1 + MID_HALO + MID_ROWS])):
+            mids_out[j, 0] = tile
+        if cycle == 0:
+            for j, tile in enumerate(pack_mid(g1[0, MID_HALO:MID_HALO + MID_ROWS])):
+                mids_out[j, 1] = tile
+        start_mid(mids_out, mids_in, sems.at[used + 6], sems.at[used + 7], near)
+        def pass_on():
+            arrived(one_in, sems.at[used + 1])
+            for part in range(wide):
+                two_send[cycle, part] = one_send[cycle, part] + jnp.sum(one_got[cycle, :, part], axis=0)
+            spread(two_out, two_in, used + 4, to_x)
+
+        if cycle > 0:
+            pass_on()
 
         arrived(l_got.at[cycle], sems.at[used + 3])
         right = i2[...] * unpack_low(tiles_of(cycle), None, None, None)
         low = right
         for turn in range(COARSE_SWEEPS - 1):
             low = right + (1.0 - relaxation) * low + low_sum(low, c2)
+        if cycle == 0:
+            mine = own_low(low)
+            for q in (0, 1):
+                l_send[3, q] = pack_low([mine[4 * q + m] for m in range(4)])
+            spread(l_send.at[3], l_got.at[3], 24, outward)
+            pass_on()
+
+        def put_u(row, a, own, tile):
+            tile = jnp.where(own, ub[0, 1 + row], tile) if a == 0 else tile
+            ub[0, 1 + row] = jnp.where(k1[0, 1 + row] > 0.0, tile, 0.0)
+
+        def put_g(row, a, own, tile):
+            tile = jnp.where(own, g1[0, row], tile) if a == 0 else tile
+            g1[0, row] = jnp.where(k1[0, 1 + row] > 0.0, tile, 0.0)
+
+        arrived(mids_in, sems.at[used + 7])
+        unpack_mid(mids_in, 0, put_u)
+        if cycle == 0:
+            unpack_mid(mids_in, 1, put_g)
+            arrived(l_got.at[3], sems.at[25])
+            low = jnp.where(k2[...] > 0.0, unpack_low(tiles_of(3), None, None, None), 0.0)
 
         arrived(two_in, sems.at[used + 5])
         parts = []
@@ -510,45 +608,30 @@
                 shifts[8 * tile + i] = jnp.broadcast_to(shift[i:i + 1], (NZ, LANES))
 
         for part in (0, 1):
-            tiles = slice(6, LOW_TILES) if part == 0 else slice(0, 6)
-            moved = jnp.where(k2[tiles] > 0.0, shifts[2 + 6 * part:8 + 6 * part], 0.0)
-            wave = select_lanes(low[tiles] + moved, picked[5 + part])
-            at = 3 + 12 * part
-            ua[0, at:at + 12] = ub[0, at:at + 12] + twice_rows(wave)
-        sweep(ua, ub, c1, g1, 2, 3, 8)
-        sweep(ub, ua, c1, g1, 2, 3, 8)
-
-        for row in range(8, 48, 8):
-            wave = ua[0, row // 2 + 1:row // 2 + 5]
+            tiles = slice(4, LOW_TILES) if part == 0 else slice(0, 8)
+            moved = jnp.where(k2[tiles] > 0.0, shifts[8 * part:8 * part + 8], 0.0)
+            wave = twice_rows(select_lanes(low[tiles] + moved, picked[5 + part]))
+            at, count = (1, MID // 2) if part == 0 else (1 + MID // 2, MID // 2)
+            ua[0, at:at + count] = ub[0, at:at + count] + (wave[1:] if part == 0 else wave[:-1])
+        around = rows_1(6 if cycle == 0 else 2)
+        sweep(ua, ub, c1, g1, *around)
+        sweep(ub, ua, c1, g1, *around)
+
+        for row, rows in groups(*rows_0(10 if cycle == 0 else 2)):
+            wave = ua[0, row // 2 + 1:(row + rows) // 2 + 1]
+            here = slice(row + 1, row + rows + 1)
             for t in (0, 1):
-                spare[t, row + 1:row + 9] = fine[t, row + 1:row + 9] + twice_rows(
-                    select_lanes(wave, picked[2 + t]))
-        sweep(spare, fine, c0, g0, 8, 5, 8)
-        for part in range(ROWS // 8):
-            row = HALO + 8 * part
-            old, total = weighted(fine, c0, row, 8, (0,))
-            s_own[8 * part:8 * part + 8] = (
-                g0[0, row:row + 8] + (1.0 - relaxation) * old[0] + total[0])
-        used += 6
-
+                spare[t, here] = fine[t, here] + twice_rows(select_lanes(wave, picked[2 + t]))
         if cycle < CYCLES - 1:
-            FOR_S.stage(s_edge, s_own)
-            FOR_S.start(s_own, s_edge, s_got, sems.at[used], sems.at[used + 1], near)
-            va[0, 1 + HALO:1 + HALO + ROWS] = s_own[...]
-            va[0, 1] = zero
-            va[0, FINE] = zero
-
-            def put_s_rows(first, rows, values):
-                inside = k0[0, 1 + first:1 + first + rows] > 0.0
-                va[0, 1 + first:1 + first + rows] = jnp.where(inside, values, 0.0)
-
-            def put_s_beside(i, tile):
-                va[1, 1 + i] = jnp.where(k0[1, 1 + i] > 0.0, tile, 0.0)
-
-            arrived(s_got, sems.at[used + 1])
-            FOR_S.unpack(s_got, put_s_rows, put_s_beside)
-            arrived(s_got, sems.at[used])
-            used += 2
+            sweep(spare, fine, c0, g0, *rows_0(8))
+            sweep(fine, spare, c0, g0, *rows_0(8))
+        else:
+            sweep(spare, fine, c0, g0, *rows_0(1))
+            for row, rows in groups(*rows_0(0)):
+                old, total = weighted(fine, c0, row, rows, (0,))
+                s_own[row - HALO:row - HALO + rows] = (
+                    g0[0, row:row + rows] + (1.0 - relaxation) * old[0] + total[0])
+        used += 8
 
     for r in range(ROWS):
         out_ref[pl.ds(r, NZ, stride=ROWS), :] = s_own[r]
@@ -556,6 +639,9 @@
     arrived(l_got.at[2], sems.at[2])
     arrived(k_got, sems.at[4])
     arrived(f_got, sems.at[6])
+    arrived(l_got.at[3], sems.at[24])
+    arrived(m_got, sems.at[14])
+    arrived(n_got, sems.at[22])
     for cycle, at in ((0, 8), (1, 16)):
         wide = pl.ds(0, 2 - cycle)
         arrived(one_got.at[cycle, :, wide], sems.at[at])
@@ -570,23 +656,24 @@
 def shards(source, coefficient, strip_rows):
     size_x, size_y = lax.axis_size("px"), lax.axis_size("py")
     flat = (NZ * ROWS, LANES)
-    scratch = [pltpu.VMEM(flat, jnp.float32)] * 2
-    scratch += [vmem(ROWS), vmem(ROWS), vmem(ROWS), vmem(2, 4), vmem(2, 4), vmem(2, 4)]
-    scratch += [vmem(e.at[8]) for e in (FOR_K, FOR_F, FOR_S)]
+    scratch = [pltpu.SMEM(strip_rows.shape, jnp.int32)] + [pltpu.VMEM(flat, jnp.float32)] * 2
+    scratch += [vmem(ROWS), vmem(ROWS), vmem(ROWS), vmem(2, 4), vmem(2, 4)]
+    scratch += [vmem(e.at[8]) for e in (FOR_K, FOR_F)]
     scratch += [vmem(2, FINE + 2), vmem(6, 2, FINE), vmem(2, FINE), vmem(2, FINE)]
     scratch += [vmem(2, FINE + 2), vmem(2, FINE + 2)]
     scratch += [vmem(1, MID + 2), vmem(6, 1, MID), vmem(1, MID), vmem(1, MID), vmem(1, MID)]
     scratch += [vmem(1, MID + 2), vmem(1, MID + 2)]
     scratch += [vmem(LOW_TILES), vmem(6, 1, LOW_TILES), vmem(LOW_TILES)]
-    scratch += [vmem(OWN2), vmem(16), vmem(2), vmem(OWN2), vmem(3, 2), vmem(3, 8, 2)]
+    scratch += [vmem(OWN2), vmem(16), vmem(2), vmem(OWN2), vmem(4, 2), vmem(4, 8, 2)]
+    scratch += [vmem(MID_ROWS // 2, 2), vmem(MID_TILES, 2), vmem(MID_ROWS // 2, 1), vmem(MID_TILES, 1)]
     row = lambda *shape: pltpu.VMEM(shape + (1, LANES), jnp.float32)
     scratch += [row(2, 2), row(2, size_y - 1, 2), row(2, 2), row(2, size_x - 1, 2)]
-    scratch += [pltpu.VMEM((8, LANES, LANES), jnp.float32), pltpu.SemaphoreType.DMA((22,))]
+    scratch += [pltpu.VMEM((8, LANES, LANES), jnp.float32), pltpu.SemaphoreType.DMA((27,))]
     hbm = pl.BlockSpec(memory_space=pltpu.HBM)
     done = pl.pallas_call(
         kernel,
         out_shape=jax.ShapeDtypeStruct(flat, jnp.float32),
-        in_specs=[pl.BlockSpec(memory_space=pltpu.SMEM), hbm, hbm],
+        in_specs=[hbm, hbm, hbm],
         out_specs=pl.BlockSpec(memory_space=pltpu.VMEM),
         scratch_shapes=scratch,
         compiler_params=pltpu.CompilerParams(

time: 49.7 us -> 47.3 us (0.952)
  Pallas kernels: 46.5 us -> 44.1 us
    pallas_call x1, Pallas kernels: 46.5 us -> 44.1 us  [shards(): pl.pallas_call(kernel, out_shape=jax.ShapeDtypeStruct(flat, jnp.float32),...]
where the time goes in v3:
time: 47.3 us; the launch traced here: 47.2 us
  Pallas kernels  44.1 us (93%)
  local copies, waits for them, and re-layouts  3.12 us (7%)
    pallas_call x1, Pallas kernels, shards(): pl.pallas_call(kernel, out_shape=jax.ShapeDtypeStruct(flat, jnp.float32),...  44.1 us
    unnamed x7, local copies, waits for them, and re-layouts  3.12 us

profile of v3, /device:TPU:1, one launch (start us, length us, event | category | flops | bytes accessed | tf_op | source)
XLA Modules:
  0.0 47.2 jit_solution(7314030032297098610)
XLA Ops:
  0.0 0.0 copy-start.2
  0.0 0.7 %copy-done.2 = s32[16]{0:T(128)S(1)} copy-done((s32[16]{0:T(128)S(1)}, s32[16]{0:T(128)}, u32[]{:S(2)}) %copy-start.2) | copy-done | bytes 88
  0.7 0.0 copy-start
  0.7 0.9 %copy-done = f32[8,32,128]{2,1,0:T(8,128)S(1)} copy-done((f32[8,32,128]{2,1,0:T(8,128)S(1)}, f32[8,32,128]{2,1,0:T(8,128)}, u32[]{:S(2)}) %copy-start) | copy-done | bytes 131096
  1.6 0.0 copy-start.1
  1.6 0.9 %copy-done.1 = f32[8,32,128]{2,1,0:T(8,128)S(1)} copy-done((f32[8,32,128]{2,1,0:T(8,128)S(1)}, f32[8,32,128]{2,1,0:T(8,128)}, u32[]{:S(2)}) %copy-start.1) | copy-done | bytes 131096
  2.5 44.1 %cycles.1 = f32[256,128]{1,0:T(8,128)S(1)} custom-call(s32[16]{0:T(128)S(1)} %copy-done.2, f32[256,128]{1,0:T(8,128)S(1)} %bitcast.4, f32[256,128]{1,0:T(8,128)S(1)} %bitcast.5), custom_call_target="tpu_custom_call" | custom-call | tf_op jit(solution)/shard_map/cycles/pallas_call | solution.py:673
  46.5 0.7 %copy.5 = f32[8,32,128]{2,1,0:T(8,128)} copy(f32[8,32,128]{2,1,0:T(8,128)S(1)} %bitcast.3) | data formatting | bytes 262144
Async XLA Ops:
  0.0 0.7 %copy-start.2 = (s32[16]{0:T(128)S(1)}, s32[16]{0:T(128)}, u32[]{:S(2)}) copy-start(s32[16]{0:T(128)} %strip_hbm.1) | copy-start | bytes 196
  0.7 0.9 %copy-start = (f32[8,32,128]{2,1,0:T(8,128)S(1)}, f32[8,32,128]{2,1,0:T(8,128)}, u32[]{:S(2)}) copy-start(f32[8,32,128]{2,1,0:T(8,128)} %param.3) | copy-start | bytes 393220
  1.6 0.9 %copy-start.1 = (f32[8,32,128]{2,1,0:T(8,128)S(1)}, f32[8,32,128]{2,1,0:T(8,128)}, u32[]{:S(2)}) copy-start(f32[8,32,128]{2,1,0:T(8,128)} %param.4) | copy-start | bytes 393220

commit v4 on v3

--- a/solution.py
+++ b/solution.py
@@ -20,9 +20,10 @@
 FINE = ROWS + 2 * HALO
 MID = FINE // 2
 OWN2 = ROWS // 4
-LOW_TILES = 3 * OWN2 // 2
+LOW_HALO = 10
+LOW_TILES = (OWN2 + 2 * LOW_HALO) // 2
 MID_LANE, MID_OWN = 32, 64
-LOW_LANE, LOW_OWN, HALF = 8, 32, 64
+LOW_LANE, LOW_OWN, HALF = LOW_HALO, 32, 64
 MID_HALO, MID_ROWS = HALO // 2, ROWS // 2
 
 
@@ -175,24 +176,26 @@
 def unpack_low(get, scale_left, scale_right, scale_rows):
     lane = lax.broadcasted_iota(jnp.int32, (NZ, LANES), 1)
     rows = []
-    for a in (-1, 0, 1):
-        for q in (0, 1):
-            own = get(a, 0, q)
-            left, right = roll_lanes(get(a, -1, q), -LOW_OWN), roll_lanes(get(a, 1, q), LOW_OWN)
-            if scale_left is not None:
-                left, right = left * scale_left, right * scale_right
-            if scale_rows is not None and a != 0:
-                scale = scale_rows[0 if a < 0 else 1]
-                own, left, right = own * scale, left * scale, right * scale
-            for m in range(4):
-                row = len(rows)
-                away = (lane - LOW_OWN * m) % LANES
-                tile = jnp.where(
-                    away < LOW_OWN, own,
-                    jnp.where(away < LOW_OWN + LOW_LANE, right,
-                              jnp.where(away >= LANES - LOW_LANE, left, 0.0)))
-                half = HALF if row >= LOW_TILES else 0
-                rows.append(roll_lanes(tile, half + LOW_LANE - LOW_OWN * m))
+    far = LOW_HALO - OWN2
+    parts = [(-2, 1, range(4 - far, 4)), (2, 0, range(far))]
+    parts[1:1] = [(a, q, range(4)) for a in (-1, 0, 1) for q in (0, 1)]
+    for a, q, members in parts:
+        own = get(a, 0, q)
+        left, right = roll_lanes(get(a, -1, q), -LOW_OWN), roll_lanes(get(a, 1, q), LOW_OWN)
+        if scale_left is not None:
+            left, right = left * scale_left, right * scale_right
+        if scale_rows is not None and a != 0:
+            scale = scale_rows[a]
+            own, left, right = own * scale, left * scale, right * scale
+        for m in members:
+            row = len(rows)
+            away = (lane - LOW_OWN * m) % LANES
+            tile = jnp.where(
+                away < LOW_OWN, own,
+                jnp.where(away < LOW_OWN + LOW_LANE, right,
+                          jnp.where(away >= LANES - LOW_LANE, left, 0.0)))
+            half = HALF if row >= LOW_TILES else 0
+            rows.append(roll_lanes(tile, half + LOW_LANE - LOW_OWN * m))
     return jnp.stack([rows[i] + rows[i + LOW_TILES] for i in range(LOW_TILES)])
 
 
@@ -207,6 +210,25 @@
 for side in [(a, b) for a in (-1, 0, 1) for b in (-1, 0, 1) if (a, b) != (0, 0)]:
     MID_AT[side] = MID_TILES
     MID_TILES += MID_ROWS // 2 if side[0] == 0 else MID_ROWS // 4
+
+
+LOW_AT, LOW_COUNT = {}, 0
+for side in [(a, b) for a in (-2, 2, -1, 1, 0) for b in (-1, 1, 0) if (a, b) != (0, 0)]:
+    LOW_AT[side] = LOW_COUNT
+    LOW_COUNT += 1 if abs(side[0]) == 2 else 2
+
+
+def start_low(send, got, send_sem, got_sem, near):
+    for (a, b), at in LOW_AT.items():
+        tiles, first = (1, 1 if a < 0 else 0) if abs(a) == 2 else (2, 0)
+        pltpu.make_async_remote_copy(
+            src_ref=send.at[pl.ds(first, tiles)],
+            dst_ref=got.at[pl.ds(at, tiles)],
+            send_sem=send_sem,
+            recv_sem=got_sem,
+            device_id=near(-a, -b),
+            device_id_type=MESH,
+        ).start()
 
 
 def start_mid(send, got, send_sem, got_sem, near):
@@ -248,7 +270,7 @@
             for group in range(4):
                 edges[side, group] = pack_edges(block, group, side == 1)
 
-    def start(self, block, edges, got, send_sem, got_sem, near):
+    def start(self, block, edges, got, send_sem, got_sem, near, rows):
         n, at = self.depth, self.at
         top, bottom = pl.ds(0, 2), pl.ds(2, 2)
         moves = [
@@ -261,7 +283,7 @@
             (edges.at[1, top], 6, (-1, 1)),
             (edges.at[0, top], 7, (-1, -1)),
         ]
-        for source, slot, way in moves:
+        for source, slot, way in moves[:2] if rows else moves[:3:-1] + moves[2:4]:
             pltpu.make_async_remote_copy(
                 src_ref=source,
                 dst_ref=got.at[pl.ds(at[slot], at[slot + 1] - at[slot])],
@@ -320,7 +342,8 @@
         range(1, size_x),
         key=lambda a: -around_ring(a % 4, 4) - around_ring((a + 1) // 4, size_x // 4))
     to_y, to_x = [(0, b) for b in along_y], [(a, 0) for a in along_x]
-    peers = to_y + to_x + [way for way in AROUND if way[0] and way[1]]
+    peers = [(a, b) for a in (-2, 2) for b in (-1, 1)] + to_y + to_x
+    peers += [way for way in AROUND if way[0] and way[1]]
     barrier = pltpu.get_barrier_semaphore()
     for way in peers:
         pl.semaphore_signal(barrier, inc=1, device_id=near(*way), device_id_type=MESH)
@@ -352,7 +375,7 @@
     def low_of(mid, half):
         return half + LOW_LANE - MID_LANE // 2 + mid // 2
 
-    mid_halo = 2 * LOW_LANE
+    mid_halo = EDGE
     mid_in = (other >= MID_LANE - mid_halo) & (other < MID_LANE + MID_OWN + mid_halo)
     tables = [
         chosen(other == MID_LANE + one // 2), chosen(beside_pairs(one, other)),
@@ -398,28 +421,31 @@
     k_copy.wait()
     for r in range(ROWS):
         k_own[r] = k_in[pl.ds(r, NZ, stride=ROWS), :]
+    pl.semaphore_wait(barrier, len(peers))
+    FOR_K.start(k_own, k_edge, k_got, sems.at[4], sems.at[5], near, True)
     lows = (1.0 / 16.0) * select_lanes(pair_rows(pair_rows(k_own[...])), picked[7])
+    FOR_K.stage(k_edge, k_own)
+    FOR_K.start(k_own, k_edge, k_got, sems.at[4], sems.at[5], near, False)
     for q in (0, 1):
         l_send[2, q] = pack_low([lows[4 * q + m] for m in range(4)])
-    FOR_K.stage(k_edge, k_own)
+    start_low(l_send.at[2], l_got.at[2], sems.at[2], sems.at[3], near)
     f_copy.wait()
     for r in range(ROWS):
         f_own[r] = f_in[pl.ds(r, NZ, stride=ROWS), :]
+    FOR_F.start(f_own, f_edge, f_got, sems.at[6], sems.at[7], near, True)
     FOR_F.stage(f_edge, f_own)
-    pl.semaphore_wait(barrier, len(peers))
-    outward = [(-a, -b) for a, b in AROUND]
-    spread(l_send.at[2], l_got.at[2], 2, outward)
-    FOR_K.start(k_own, k_edge, k_got, sems.at[4], sems.at[5], near)
-    FOR_F.start(f_own, f_edge, f_got, sems.at[6], sems.at[7], near)
+    FOR_F.start(f_own, f_edge, f_got, sems.at[6], sems.at[7], near, False)
 
     wide_lane = lax.broadcasted_iota(jnp.int32, (NZ, LANES), 1)
     in_left, in_right = jnp.where(py > 0, 1.0, 0.0), jnp.where(py < size_y - 1, 1.0, 0.0)
     inner_y = jnp.where(wide_lane < LANES // 2, in_right, in_left)
     row_in = [jnp.where(px > 0, 1.0, 0.0), jnp.where(px < size_x - 1, 1.0, 0.0)]
+    low_in = {-1: row_in[0], 1: row_in[1], -2: jnp.where(px > 1, 1.0, 0.0),
+              2: jnp.where(px < size_x - 2, 1.0, 0.0)}
 
     kept = []
     for tile in range(4):
-        rows = OWN2 * px - OWN2 + 8 * tile + sub
+        rows = OWN2 * px - LOW_HALO + 8 * tile + sub
         flags = jnp.ones((8, LANES), jnp.float32)
         for end in ends:
             flags = jnp.where(rows == end, 0.0, flags)
@@ -430,11 +456,15 @@
                    for i in range(LOW_TILES)]) for d in (0, 1)]
 
     def tiles_of(at):
-        return lambda a, b, q: (
-            l_send[at, q] if (a, b) == (0, 0) else l_got[at, AROUND.index((a, b)), q])
+        def get(a, b, q):
+            if (a, b) == (0, 0):
+                return l_send[at, q]
+            return l_got[at, LOW_AT[a, b] + (0 if abs(a) == 2 else q)]
+
+        return get
 
     arrived(l_got.at[2], sems.at[3])
-    lows = unpack_low(tiles_of(2), in_left, in_right, row_in)
+    lows = unpack_low(tiles_of(2), in_left, in_right, low_in)
     k2[...] = lows
     west, east = low_rows_beside(lows)
     faces, inverse, diagonal = scaled_faces(
@@ -449,7 +479,7 @@
 
     def own_low(values):
         out = []
-        for r in range(OWN2, 2 * OWN2):
+        for r in range(LOW_HALO, LOW_HALO + OWN2):
             half = HALF if r >= LOW_TILES else 0
             moved = roll_lanes(values[r % LOW_TILES], -half - LOW_LANE)
             out.append(jnp.where(wide_lane < LOW_OWN, moved, 0.0))
@@ -550,7 +580,7 @@
         spread(one_out, one_in, used, to_y)
         for q in (0, 1):
             l_send[cycle, q] = pack_low([l_own[4 * q + m] for m in range(4)])
-        spread(l_send.at[cycle], l_got.at[cycle], used + 2, outward)
+        start_low(l_send.at[cycle], l_got.at[cycle], sems.at[used + 2], sems.at[used + 3], near)
         mids_out, mids_in = (m_send, m_got) if cycle == 0 else (n_send, n_got)
         for j, tile in enumerate(pack_mid(ub[0, 1 + MID_HALO:1 + MID_HALO + MID_ROWS])):
             mids_out[j, 0] = tile
@@ -558,27 +588,16 @@
             for j, tile in enumerate(pack_mid(g1[0, MID_HALO:MID_HALO + MID_ROWS])):
                 mids_out[j, 1] = tile
         start_mid(mids_out, mids_in, sems.at[used + 6], sems.at[used + 7], near)
-        def pass_on():
-            arrived(one_in, sems.at[used + 1])
-            for part in range(wide):
-                two_send[cycle, part] = one_send[cycle, part] + jnp.sum(one_got[cycle, :, part], axis=0)
-            spread(two_out, two_in, used + 4, to_x)
-
-        if cycle > 0:
-            pass_on()
+        arrived(one_in, sems.at[used + 1])
+        for part in range(wide):
+            two_send[cycle, part] = one_send[cycle, part] + jnp.sum(one_got[cycle, :, part], axis=0)
+        spread(two_out, two_in, used + 4, to_x)
 
         arrived(l_got.at[cycle], sems.at[used + 3])
         right = i2[...] * unpack_low(tiles_of(cycle), None, None, None)
         low = right
         for turn in range(COARSE_SWEEPS - 1):
             low = right + (1.0 - relaxation) * low + low_sum(low, c2)
-        if cycle == 0:
-            mine = own_low(low)
-            for q in (0, 1):
-                l_send[3, q] = pack_low([mine[4 * q + m] for m in range(4)])
-            spread(l_send.at[3], l_got.at[3], 24, outward)
-            pass_on()
-
         def put_u(row, a, own, tile):
             tile = jnp.where(own, ub[0, 1 + row], tile) if a == 0 else tile
             ub[0, 1 + row] = jnp.where(k1[0, 1 + row] > 0.0, tile, 0.0)
@@ -591,8 +610,6 @@
         unpack_mid(mids_in, 0, put_u)
         if cycle == 0:
             unpack_mid(mids_in, 1, put_g)
-            arrived(l_got.at[3], sems.at[25])
-            low = jnp.where(k2[...] > 0.0, unpack_low(tiles_of(3), None, None, None), 0.0)
 
         arrived(two_in, sems.at[used + 5])
         parts = []
@@ -608,7 +625,7 @@
                 shifts[8 * tile + i] = jnp.broadcast_to(shift[i:i + 1], (NZ, LANES))
 
         for part in (0, 1):
-            tiles = slice(4, LOW_TILES) if part == 0 else slice(0, 8)
+            tiles = slice(LOW_TILES - 8, LOW_TILES) if part == 0 else slice(0, 8)
             moved = jnp.where(k2[tiles] > 0.0, shifts[8 * part:8 * part + 8], 0.0)
             wave = twice_rows(select_lanes(low[tiles] + moved, picked[5 + part]))
             at, count = (1, MID // 2) if part == 0 else (1 + MID // 2, MID // 2)
@@ -639,7 +656,6 @@
     arrived(l_got.at[2], sems.at[2])
     arrived(k_got, sems.at[4])
     arrived(f_got, sems.at[6])
-    arrived(l_got.at[3], sems.at[24])
     arrived(m_got, sems.at[14])
     arrived(n_got, sems.at[22])
     for cycle, at in ((0, 8), (1, 16)):
@@ -664,7 +680,7 @@
     scratch += [vmem(1, MID + 2), vmem(6, 1, MID), vmem(1, MID), vmem(1, MID), vmem(1, MID)]
     scratch += [vmem(1, MID + 2), vmem(1, MID + 2)]
     scratch += [vmem(LOW_TILES), vmem(6, 1, LOW_TILES), vmem(LOW_TILES)]
-    scratch += [vmem(OWN2), vmem(16), vmem(2), vmem(OWN2), vmem(4, 2), vmem(4, 8, 2)]
+    scratch += [vmem(OWN2), vmem(16), vmem(2), vmem(OWN2), vmem(3, 2), vmem(3, LOW_COUNT)]
     scratch += [vmem(MID_ROWS // 2, 2), vmem(MID_TILES, 2), vmem(MID_ROWS // 2, 1), vmem(MID_TILES, 1)]
     row = lambda *shape: pltpu.VMEM(shape + (1, LANES), jnp.float32)
     scratch += [row(2, 2), row(2, size_y - 1, 2), row(2, 2), row(2, size_x - 1, 2)]
@@ -677,7 +693,7 @@
         out_specs=pl.BlockSpec(memory_space=pltpu.VMEM),
         scratch_shapes=scratch,
         compiler_params=pltpu.CompilerParams(
-            collective_id=0, has_side_effects=True, vmem_limit_bytes=32 << 20
+            collective_id=0, has_side_effects=True, vmem_limit_bytes=60 << 20
         ),
         name="cycles",
     )(strip_rows, source.reshape(flat), coefficient.reshape(flat))

time: 47.3 us -> 45 us (0.951)
  local copies, waits for them, and re-layouts: 3.12 us -> 1.57 us
  Pallas kernels: 44.1 us -> 43.3 us
    unnamed x7 -> x1, local copies, waits for them, and re-layouts: 3.12 us -> 1.57 us
    pallas_call x1, Pallas kernels: 44.1 us -> 43.3 us  [shards(): pl.pallas_call(kernel, out_shape=jax.ShapeDtypeStruct(flat, jnp.float32),...]
where the time goes in v4:
time: 45 us; the launch traced here: 44.9 us
  Pallas kernels  43.3 us (96%)
  local copies, waits for them, and re-layouts  1.57 us (3%)
    pallas_call x1, Pallas kernels, shards(): pl.pallas_call(kernel, out_shape=jax.ShapeDtypeStruct(flat, jnp.float32),...  43.3 us
    unnamed x1, local copies, waits for them, and re-layouts  1.57 us

profile of v4, /device:TPU:1, one launch (start us, length us, event | category | flops | bytes accessed | tf_op | source)
XLA Modules:
  0.0 44.9 jit_solution(16009264644445806859)
XLA Ops:
  0.0 43.3 %cycles.1 = f32[256,128]{1,0:T(8,128)} custom-call(s32[16]{0:T(128)} %strip_hbm.1, f32[256,128]{1,0:T(8,128)} %bitcast.4, f32[256,128]{1,0:T(8,128)} %bitcast.5), custom_call_target="tpu_custom_call" | custom-call | tf_op jit(solution)/shard_map/cycles/pallas_call | solution.py:689
  43.3 1.6 %copy.5 = f32[8,32,128]{2,1,0:T(8,128)} copy(f32[8,32,128]{2,1,0:T(8,128)} %bitcast.3) | data formatting | bytes 262144

commit v5 on v4

--- a/solution.py
+++ b/solution.py
@@ -270,7 +270,7 @@
             for group in range(4):
                 edges[side, group] = pack_edges(block, group, side == 1)
 
-    def start(self, block, edges, got, send_sem, got_sem, near, rows):
+    def start(self, block, edges, got, send_sem, got_sem, near):
         n, at = self.depth, self.at
         top, bottom = pl.ds(0, 2), pl.ds(2, 2)
         moves = [
@@ -283,7 +283,7 @@
             (edges.at[1, top], 6, (-1, 1)),
             (edges.at[0, top], 7, (-1, -1)),
         ]
-        for source, slot, way in moves[:2] if rows else moves[:3:-1] + moves[2:4]:
+        for source, slot, way in moves[4:] + moves[:4]:
             pltpu.make_async_remote_copy(
                 src_ref=source,
                 dst_ref=got.at[pl.ds(at[slot], at[slot + 1] - at[slot])],
@@ -421,20 +421,18 @@
     k_copy.wait()
     for r in range(ROWS):
         k_own[r] = k_in[pl.ds(r, NZ, stride=ROWS), :]
-    pl.semaphore_wait(barrier, len(peers))
-    FOR_K.start(k_own, k_edge, k_got, sems.at[4], sems.at[5], near, True)
     lows = (1.0 / 16.0) * select_lanes(pair_rows(pair_rows(k_own[...])), picked[7])
-    FOR_K.stage(k_edge, k_own)
-    FOR_K.start(k_own, k_edge, k_got, sems.at[4], sems.at[5], near, False)
     for q in (0, 1):
         l_send[2, q] = pack_low([lows[4 * q + m] for m in range(4)])
-    start_low(l_send.at[2], l_got.at[2], sems.at[2], sems.at[3], near)
+    FOR_K.stage(k_edge, k_own)
     f_copy.wait()
     for r in range(ROWS):
         f_own[r] = f_in[pl.ds(r, NZ, stride=ROWS), :]
-    FOR_F.start(f_own, f_edge, f_got, sems.at[6], sems.at[7], near, True)
     FOR_F.stage(f_edge, f_own)
-    FOR_F.start(f_own, f_edge, f_got, sems.at[6], sems.at[7], near, False)
+    pl.semaphore_wait(barrier, len(peers))
+    start_low(l_send.at[2], l_got.at[2], sems.at[2], sems.at[3], near)
+    FOR_K.start(k_own, k_edge, k_got, sems.at[4], sems.at[5], near)
+    FOR_F.start(f_own, f_edge, f_got, sems.at[6], sems.at[7], near)
 
     wide_lane = lax.broadcasted_iota(jnp.int32, (NZ, LANES), 1)
     in_left, in_right = jnp.where(py > 0, 1.0, 0.0), jnp.where(py < size_y - 1, 1.0, 0.0)

time: 45 us -> 44 us (0.978)
  Pallas kernels: 43.3 us -> 42.3 us
    pallas_call x1, Pallas kernels: 43.3 us -> 42.3 us  [shards(): pl.pallas_call(kernel, out_shape=jax.ShapeDtypeStruct(flat, jnp.float32),...]
where the time goes in v5:
time: 44 us; the launch traced here: 43.9 us
  Pallas kernels  42.3 us (96%)
  local copies, waits for them, and re-layouts  1.57 us (4%)
    pallas_call x1, Pallas kernels, shards(): pl.pallas_call(kernel, out_shape=jax.ShapeDtypeStruct(flat, jnp.float32),...  42.3 us
    unnamed x1, local copies, waits for them, and re-layouts  1.57 us

profile of v5, /device:TPU:1, one launch (start us, length us, event | category | flops | bytes accessed | tf_op | source)
XLA Modules:
  0.0 43.9 jit_solution(13657922182229096954)
XLA Ops:
  0.0 42.3 %cycles.1 = f32[256,128]{1,0:T(8,128)} custom-call(s32[16]{0:T(128)} %strip_hbm.1, f32[256,128]{1,0:T(8,128)} %bitcast.4, f32[256,128]{1,0:T(8,128)} %bitcast.5), custom_call_target="tpu_custom_call" | custom-call | tf_op jit(solution)/shard_map/cycles/pallas_call | solution.py:687
  42.3 1.6 %copy.5 = f32[8,32,128]{2,1,0:T(8,128)} copy(f32[8,32,128]{2,1,0:T(8,128)} %bitcast.3) | data formatting | bytes 262144

commit v6 on v5

--- a/solution.py
+++ b/solution.py
@@ -686,7 +686,7 @@
     hbm = pl.BlockSpec(memory_space=pltpu.HBM)
     done = pl.pallas_call(
         kernel,
-        out_shape=jax.ShapeDtypeStruct(flat, jnp.float32),
+        out_shape=pltpu.VMEM(flat, jnp.float32),
         in_specs=[hbm, hbm, hbm],
         out_specs=pl.BlockSpec(memory_space=pltpu.VMEM),
         scratch_shapes=scratch,

time: 44 us -> 42.4 us (0.964)
  local copies, waits for them, and re-layouts: 1.57 us -> 0.66 us
  Pallas kernels: 42.3 us -> 41.7 us
    unnamed x1, local copies, waits for them, and re-layouts: 1.57 us -> 0.66 us
    pallas_call x1, Pallas kernels: 42.3 us -> 41.7 us  [shards(): pl.pallas_call(kernel, out_shape=pltpu.VMEM(flat, jnp.float32), in_specs=...]
where the time goes in v6:
time: 42.4 us; the launch traced here: 42.3 us
  Pallas kernels  41.7 us (98%)
  local copies, waits for them, and re-layouts  0.66 us (2%)
    pallas_call x1, Pallas kernels, shards(): pl.pallas_call(kernel, out_shape=pltpu.VMEM(flat, jnp.float32), in_specs=...  41.7 us

profile of v6, /device:TPU:1, one launch (start us, length us, event | category | flops | bytes accessed | tf_op | source)
XLA Modules:
  0.0 42.3 jit_solution(9506690339354585615)
XLA Ops:
  0.0 41.7 %cycles.1 = f32[256,128]{1,0:T(8,128)S(1)} custom-call(s32[16]{0:T(128)} %strip_hbm.1, f32[256,128]{1,0:T(8,128)} %bitcast.4, f32[256,128]{1,0:T(8,128)} %bitcast.5), custom_call_target="tpu_custom_call" | custom-call | tf_op jit(solution)/shard_map/cycles/pallas_call | solution.py:687
  41.7 0.7 %copy.5 = f32[8,32,128]{2,1,0:T(8,128)} copy(f32[8,32,128]{2,1,0:T(8,128)S(1)} %bitcast.3) | data formatting | bytes 262144

commit v7 on v6

--- a/solution.py
+++ b/solution.py
@@ -317,7 +317,7 @@
 
 
 def kernel(strip_hbm, source_ref, coefficient_ref, out_ref,
-           strip_ref, k_in, f_in, k_own, f_own, s_own, k_edge, f_edge, k_got, f_got,
+           strip_ref, k_in, f_in, k_own, f_own, k_edge, f_edge, k_got, f_got,
            k0, c0, g0, d0, va, vb, k1, c1, i1, g1, d1, ua, ub, k2, c2, i2,
            weight, shifts, pick, l_own, l_send, l_got, m_send, m_got, n_send, n_got, one_send, one_got, two_send, two_got,
            picked, sems):
@@ -472,9 +472,6 @@
         c2[side, 0] = faces[side]
     i2[...] = inverse
     ones = jnp.where(lows > 0.0, 1.0, 0.0)
-    for turn in range(COARSE_SWEEPS):
-        ones = (1.0 - relaxation) * ones + low_sum(ones, c2)
-
     def own_low(values):
         out = []
         for r in range(LOW_HALO, LOW_HALO + OWN2):
@@ -483,8 +480,6 @@
             out.append(jnp.where(wide_lane < LOW_OWN, moved, 0.0))
         return jnp.stack(out)
 
-    weight[...] = own_low(ones)
-
     def in_row(values):
         column = jnp.sum(jnp.sum(values, axis=1), axis=1, keepdims=True)
         return jnp.sum(jnp.where(lane == OWN2 * px + sub, column, 0.0), axis=0, keepdims=True)
@@ -511,11 +506,16 @@
     for row, rows in groups(0, FINE, 10):
         k1[0, row // 2 + 1:(row + rows) // 2 + 1] = 0.25 * restrict(
             [k0[t, row + 1:row + rows + 1] for t in (0, 1)])
+    turns = COARSE_SWEEPS
     for row, rows in groups(THIN, FINE - THIN):
+        if turns > 0:
+            ones = (1.0 - relaxation) * ones + low_sum(ones, c2)
+            turns -= 1
         inverse, diagonal = make_weights(k0, c0, row, rows, z_coupling)
         for t in (0, 1):
             g0[t, row:row + rows] = inverse[t]
             d0[t, row:row + rows] = (1.0 / relaxation) * diagonal[t]
+    weight[...] = own_low(ones)
     for row, rows in groups(0, MID, 10):
         inverse, diagonal = make_weights(k1, c1, row, rows, 4.0 * z_coupling)
         i1[0, row:row + rows] = inverse[0]
@@ -644,12 +644,10 @@
             sweep(spare, fine, c0, g0, *rows_0(1))
             for row, rows in groups(*rows_0(0)):
                 old, total = weighted(fine, c0, row, rows, (0,))
-                s_own[row - HALO:row - HALO + rows] = (
-                    g0[0, row:row + rows] + (1.0 - relaxation) * old[0] + total[0])
+                done = g0[0, row:row + rows] + (1.0 - relaxation) * old[0] + total[0]
+                for r in range(rows):
+                    out_ref[pl.ds(row - HALO + r, NZ, stride=ROWS), :] = done[r]
         used += 8
-
-    for r in range(ROWS):
-        out_ref[pl.ds(r, NZ, stride=ROWS), :] = s_own[r]
 
     arrived(l_got.at[2], sems.at[2])
     arrived(k_got, sems.at[4])
@@ -671,7 +669,7 @@
     size_x, size_y = lax.axis_size("px"), lax.axis_size("py")
     flat = (NZ * ROWS, LANES)
     scratch = [pltpu.SMEM(strip_rows.shape, jnp.int32)] + [pltpu.VMEM(flat, jnp.float32)] * 2
-    scratch += [vmem(ROWS), vmem(ROWS), vmem(ROWS), vmem(2, 4), vmem(2, 4)]
+    scratch += [vmem(ROWS), vmem(ROWS), vmem(2, 4), vmem(2, 4)]
     scratch += [vmem(e.at[8]) for e in (FOR_K, FOR_F)]
     scratch += [vmem(2, FINE + 2), vmem(6, 2, FINE), vmem(2, FINE), vmem(2, FINE)]
     scratch += [vmem(2, FINE + 2), vmem(2, FINE + 2)]

time: 42.4 us -> 42.3 us (level)
  no operation moved by 1% of the time
where the time goes in v7:
time: 42.3 us; the launch traced here: 42.2 us
  Pallas kernels  41.6 us (98%)
  local copies, waits for them, and re-layouts  0.66 us (2%)
    pallas_call x1, Pallas kernels, shards(): pl.pallas_call(kernel, out_shape=pltpu.VMEM(flat, jnp.float32), in_specs=...  41.6 us

profile of v7, /device:TPU:1, one launch (start us, length us, event | category | flops | bytes accessed | tf_op | source)
XLA Modules:
  0.0 42.2 jit_solution(13435058056612484848)
XLA Ops:
  0.0 41.6 %cycles.1 = f32[256,128]{1,0:T(8,128)S(1)} custom-call(s32[16]{0:T(128)} %strip_hbm.1, f32[256,128]{1,0:T(8,128)} %bitcast.4, f32[256,128]{1,0:T(8,128)} %bitcast.5), custom_call_target="tpu_custom_call" | custom-call | tf_op jit(solution)/shard_map/cycles/pallas_call | solution.py:685
  41.6 0.7 %copy.5 = f32[8,32,128]{2,1,0:T(8,128)} copy(f32[8,32,128]{2,1,0:T(8,128)S(1)} %bitcast.3) | data formatting | bytes 262144
